TPU v7x, 512 devices: a whole 4x4x16 slice. The times are simulated.
512 devices in a mesh: expert: 128 (over z, y, core), help: 4 (over x).
Axes of the slice: x: 4, y: 4, z: 16, core: 2. Of those that a mesh axis runs over, the one named last changes fastest.
Arguments:
- act_rows: bfloat16 [65536, 1536], P(('expert', 'help')), may hold values from -1.1953125 to 1.1953125
- grad_rows: bfloat16 [65536, 4096], P(('expert', 'help')), may hold values from -1.1953125 to 1.1953125
- routing: int32 [65536], P(('expert', 'help')), may hold values from 0 to 127, as said below
- input_panel: bfloat16 [128, 1536, 512], P('expert', None, 'help'), may hold values from -0.15625 to 0.15625
- output_panel: bfloat16 [128, 4096, 1024], P('expert', None, 'help'), may hold values from -0.09375 to 0.09375
Outputs:
- scaling: float32 [128, 512, 1024], P('expert', None, 'help')
Inputs may be any that keep to these rules, and one draw needn't show every extreme that they name: `routing`: among the rows of one device (aligned blocks of 128 rows), no expert is named more than 2 times, and one expert, the same on every device, is named exactly 2 times on every device.
All inputs are finite; a program needn't handle non-finite values.
Results may differ from a plain program's by a relative error of at most 0.00083.
Values may be sent and summed in bfloat16 or wider, within the bound.
No kernel may reach another device: no remote copies, remote signals or barrier semaphores. Data moves between devices by JAX's collectives and lax.ppermute only.
A program may use at most 64 MiB of HBM per device.

v0:
```python
import functools

import jax
import jax.numpy as jnp
from jax import lax
from jax.experimental import pallas as pl
from jax.experimental.pallas import tpu as pltpu
from jax.sharding import PartitionSpec as P


CHUNK = 512
VMEM = pl.BlockSpec(memory_space=pltpu.VMEM)
SMEM = pl.BlockSpec(memory_space=pltpu.SMEM)
HBM = pl.BlockSpec(memory_space=pltpu.HBM)


def params(mib):
    return pltpu.CompilerParams(vmem_limit_bytes=int(mib * 1024 * 1024))


def shifted(values, steps):
    helpers = lax.axis_size("help")
    return lax.ppermute(values, "help", [(i, (i + steps) % helpers) for i in range(helpers)])


def pack_kernel(routing_ref, grad_ref, act_ref, send_ref, rows_ref, packed_ref, in_sems, out_sems):
    rows, (experts, slots, width) = grad_ref.shape[0], send_ref.shape
    loads, stores, base = [], [], 0
    for ref in (grad_ref, act_ref):
        for k in range(0, ref.shape[1], CHUNK):
            at = pl.ds(base + k, CHUNK)
            loads.append(pltpu.make_async_copy(ref.at[:, pl.ds(k, CHUNK)], rows_ref.at[:, at], in_sems.at[len(loads)]))
            stores.append(pltpu.make_async_copy(packed_ref.at[:, :, at], send_ref.at[:, :, at], out_sems.at[len(stores)]))
        base += ref.shape[1]
    for load in loads:
        load.start()
    across = jnp.broadcast_to(routing_ref[...], (rows, rows))
    first, second = (lax.broadcasted_iota(jnp.int32, (rows, rows), axis) for axis in (0, 1))
    earlier = jnp.where((across.T == across) & (first < second), 1.0, 0.0)
    target = routing_ref[...] * slots + jnp.sum(earlier, axis=0, keepdims=True).astype(jnp.int32)
    slot = lax.broadcasted_iota(jnp.int32, (experts * slots, rows), 0)
    pick = jnp.where(slot == target, 1.0, 0.0).astype(jnp.bfloat16)
    for i, k in enumerate(range(0, width, CHUNK)):
        loads[i].wait()
        taken = jnp.dot(pick, rows_ref[:, k : k + CHUNK], preferred_element_type=jnp.float32)
        packed_ref[:, :, k : k + CHUNK] = taken.astype(jnp.bfloat16).reshape(experts, slots, CHUNK)
        stores[i].start()
    for store in stores:
        store.wait()


def squares_of(arrived_ref, panel_ref, held_ref, sems, base):
    rows, depth = arrived_ref.shape[0] * arrived_ref.shape[1], panel_ref.shape[0]
    loads = [
        pltpu.make_async_copy(panel_ref.at[pl.ds(k, CHUNK), :], held_ref.at[pl.ds(k, CHUNK), :], sems.at[s])
        for s, k in enumerate(range(0, depth, CHUNK))
    ]
    for load in loads:
        load.start()
    total = None
    for load, k in zip(loads, range(0, depth, CHUNK)):
        values = arrived_ref[:, :, base + k : base + k + CHUNK].reshape(rows, CHUNK)
        load.wait()
        term = jnp.dot(values, held_ref[k : k + CHUNK, :], preferred_element_type=jnp.float32)
        total = term if total is None else total + term
    return jnp.square(total).astype(jnp.bfloat16)


def input_kernel(base, arrived_ref, panel_ref, squares_ref, held_ref, sems):
    squares_ref[...] = squares_of(arrived_ref, panel_ref, held_ref, sems, base)


def output_kernel(me_ref, arrived_ref, panel_ref, squares_ref, held_ref, sems):
    helpers, _, width = squares_ref.shape
    squares = squares_of(arrived_ref, panel_ref, held_ref, sems, 0)
    for k in range(helpers):
        squares_ref[lax.rem(me_ref[0] + helpers - k, helpers)] = squares[:, k * width : (k + 1) * width]


def tile_kernel(helpers, me_ref, *refs):
    in_refs, out_ref, tile_ref = refs[:helpers], refs[-2], refs[-1]
    width = tile_ref.shape[1] // helpers
    me = me_ref[0]
    for j in range(helpers):
        total = None
        for k in range(helpers):
            block = (j + k) % helpers
            term = lax.dot_general(
                in_refs[k][:, block * width : (block + 1) * width],
                out_ref[lax.rem(me + k, helpers)],
                (((0,), (0,)), ((), ())),
                preferred_element_type=jnp.float32,
            )
            total = term if total is None else total + term
        start = pl.multiple_of(lax.rem(me + helpers - j, helpers) * width, width)
        tile_ref[0, pl.ds(start, width), :] = total


def on_device(act_rows, grad_rows, routing, input_panel, output_panel):
    experts, helpers = lax.axis_size("expert"), lax.axis_size("help")
    (row_count, width_in), width_out = act_rows.shape, grad_rows.shape[1]
    part_in, part_out = input_panel.shape[2], output_panel.shape[2]
    panel_in = part_in * helpers
    chunks, slots = (width_in + width_out) // CHUNK, 2

    send = pl.pallas_call(
        pack_kernel,
        out_shape=jax.ShapeDtypeStruct((experts, slots, width_in + width_out), jnp.bfloat16),
        in_specs=[VMEM, HBM, HBM],
        out_specs=HBM,
        scratch_shapes=[
            pltpu.VMEM((row_count, width_in + width_out), jnp.bfloat16),
            pltpu.VMEM((experts, slots, width_in + width_out), jnp.bfloat16),
            pltpu.SemaphoreType.DMA((chunks,)),
            pltpu.SemaphoreType.DMA((chunks,)),
        ],
        compiler_params=params(62),
        name="pack",
    )(routing[None, :], grad_rows, act_rows)
    arrived = lax.all_to_all(send, "expert", split_axis=0, concat_axis=0, tiled=True)

    in_parts = [input_panel[0]] + [shifted(input_panel[0], k) for k in range(1, helpers)]
    out_parts = [output_panel[0]] + [shifted(output_panel[0], k) for k in range(1, helpers)]
    joined_in, joined_out = jnp.concatenate(in_parts, axis=1), jnp.concatenate(out_parts, axis=1)
    joined_in, joined_out, arrived = lax.optimization_barrier((joined_in, joined_out, arrived))

    own_in = pl.pallas_call(
        functools.partial(input_kernel, width_out),
        out_shape=jax.ShapeDtypeStruct((slots * experts, panel_in), jnp.bfloat16),
        in_specs=[VMEM, HBM],
        out_specs=VMEM,
        scratch_shapes=[
            pltpu.VMEM((width_in, panel_in), jnp.bfloat16),
            pltpu.SemaphoreType.DMA((width_in // CHUNK,)),
        ],
        compiler_params=params(12),
        name="input_squares",
    )(arrived, pltpu.with_memory_space_constraint(joined_in, pltpu.HBM))
    all_in = [own_in] + [shifted(own_in, helpers - k) for k in range(1, helpers)]

    me = lax.axis_index("help").astype(jnp.int32)[None]
    own_out = pl.pallas_call(
        output_kernel,
        out_shape=jax.ShapeDtypeStruct((helpers, slots * experts, part_out), jnp.bfloat16),
        in_specs=[SMEM, VMEM, HBM],
        out_specs=VMEM,
        scratch_shapes=[
            pltpu.VMEM((width_out, part_out * helpers), jnp.bfloat16),
            pltpu.SemaphoreType.DMA((width_out // CHUNK,)),
        ],
        compiler_params=params(16),
        cost_estimate=pl.CostEstimate(
            flops=2 * slots * experts * width_out * part_out * helpers,
            bytes_accessed=2 * width_out * part_out * helpers,
            transcendentals=0,
        ),
        name="output_squares",
    )(me, arrived, pltpu.with_memory_space_constraint(joined_out, pltpu.HBM))
    all_out = lax.all_to_all(own_out, "help", split_axis=0, concat_axis=0, tiled=True)

    return pl.pallas_call(
        functools.partial(tile_kernel, helpers),
        out_shape=jax.ShapeDtypeStruct((1, panel_in, part_out), jnp.float32),
        in_specs=[SMEM] + [VMEM] * (helpers + 1),
        out_specs=VMEM,
        compiler_params=params(12),
        name="tile",
    )(me, *all_in, all_out)


def solution(mesh):
    placed = (
        P(("expert", "help"), None),
        P(("expert", "help"), None),
        P(("expert", "help")),
        P("expert", None, "help"),
        P("expert", None, "help"),
    )
    return jax.shard_map(
        on_device, mesh=mesh, in_specs=placed, out_specs=P("expert", None, "help"), check_vma=False
    )
```

profile of v0, /device:TPU:1, one launch (start us, length us, event | category | flops | bytes accessed | tf_op | source)
XLA Modules:
  0.0 188.5 jit_solution(15188232991161274039)
XLA Ops:
  0.0 4.9 %pack.1 = bf16[128,2,5632]{2,1,0:T(2,128)(2,1)} custom-call(s32[1,128]{1,0:T(1,128)} %bitcast.12, bf16[128,4096]{1,0:T(8,128)(2,1)} %grad_ref.1, bf16[128,1536]{1,0:T(8,128)(2,1)} %act_ref.1), custom_call_target="tpu_custom_call" | custom-call | tf_op jit(solution)/shard_map/pack/pallas_call | solution.py:106
  4.9 0.0 copy-start.4
  4.9 20.7 %all-to-all-start = ((bf16[128,2,5632]{2,1,0:T(2,128)(2,1)}), bf16[128,2,5632]{2,1,0:T(2,128)(2,1)S(1)}, u32[]{:S(2)}, u32[]{:S(2)}) async-start(bf16[128,2,5632]{2,1,0:T(2,128)(2,1)} %pack.1), calls=%async_computation | async-start | bytes 5767168 | tf_op jit(solution)/shard_map/all_to_all | solution.py:120
  25.6 3.2 %collective-permute-start.3 = (bf16[4096,256]{1,0:T(8,128)(2,1)}, bf16[4096,256]{1,0:T(8,128)(2,1)}, u32[]{:S(2)}, u32[]{:S(2)}) collective-permute-start(bf16[4096,256]{1,0:T(8,128)(2,1)} %bitcast.4), channel_id=1, source_target_pairs={{0,1},{1,2},{2,3},{3,0},{4,5},{5,6},{6,7},{7,4},{8,9},{9,10},{10,1... | collective-permute-start | bytes 6291464 | tf_op jit(solution)/shard_map/ppermute | solution.py:23
  28.8 4.3 %collective-permute-start.4 = (bf16[4096,256]{1,0:T(8,128)(2,1)}, bf16[4096,256]{1,0:T(8,128)(2,1)}, u32[]{:S(2)}, u32[]{:S(2)}) collective-permute-start(bf16[4096,256]{1,0:T(8,128)(2,1)} %bitcast.5), channel_id=1, source_target_pairs={{0,2},{1,3},{2,0},{3,1},{4,6},{5,7},{6,4},{7,5},{8,10},{9,11},{10,... | collective-permute-start | bytes 6291464 | tf_op jit(solution)/shard_map/ppermute | solution.py:23
  33.1 3.1 %collective-permute-start.5 = (bf16[4096,256]{1,0:T(8,128)(2,1)}, bf16[4096,256]{1,0:T(8,128)(2,1)}, u32[]{:S(2)}, u32[]{:S(2)}) collective-permute-start(bf16[4096,256]{1,0:T(8,128)(2,1)} %bitcast.6), channel_id=1, source_target_pairs={{0,3},{1,0},{2,1},{3,2},{4,7},{5,4},{6,5},{7,6},{8,11},{9,8},{10,9... | collective-permute-start | bytes 6291464 | tf_op jit(solution)/shard_map/ppermute | solution.py:23
  36.2 2.2 %collective-permute-start = (bf16[1536,128]{1,0:T(8,128)(2,1)S(1)}, bf16[1536,128]{1,0:T(8,128)(2,1)}, u32[]{:S(2)}, u32[]{:S(2)}) collective-permute-start(bf16[1536,128]{1,0:T(8,128)(2,1)S(1)} %bitcast.8), channel_id=1, source_target_pairs={{0,1},{1,2},{2,3},{3,0},{4,5},{5,6},{6,7},{7,4},{8,9},{9,10},{10,1... | collective-permute-start | bytes 1179656 | tf_op jit(solution)/shard_map/ppermute | solution.py:23
  38.4 2.8 %collective-permute-start.1 = (bf16[1536,128]{1,0:T(8,128)(2,1)S(1)}, bf16[1536,128]{1,0:T(8,128)(2,1)}, u32[]{:S(2)}, u32[]{:S(2)}) collective-permute-start(bf16[1536,128]{1,0:T(8,128)(2,1)S(1)} %bitcast.9), channel_id=1, source_target_pairs={{0,2},{1,3},{2,0},{3,1},{4,6},{5,7},{6,4},{7,5},{8,10},{9,11},{10,... | collective-permute-start | bytes 1179656 | tf_op jit(solution)/shard_map/ppermute | solution.py:23
  41.2 87.5 %collective-permute-done = bf16[1536,128]{1,0:T(8,128)(2,1)} collective-permute-done((bf16[1536,128]{1,0:T(8,128)(2,1)S(1)}, bf16[1536,128]{1,0:T(8,128)(2,1)}, u32[]{:S(2)}, u32[]{:S(2)}) %collective-permute-start) | collective-permute-done | bytes 393248 | tf_op jit(solution)/shard_map/ppermute | solution.py:23
  128.7 3.2 %collective-permute-start.2 = (bf16[1536,128]{1,0:T(8,128)(2,1)S(1)}, bf16[1536,128]{1,0:T(8,128)(2,1)}, u32[]{:S(2)}, u32[]{:S(2)}) collective-permute-start(bf16[1536,128]{1,0:T(8,128)(2,1)S(1)} %bitcast.10), channel_id=1, source_target_pairs={{0,3},{1,0},{2,1},{3,2},{4,7},{5,4},{6,5},{7,6},{8,11},{9,8},{10,9... | collective-permute-start | bytes 1179656 | tf_op jit(solution)/shard_map/ppermute | solution.py:23
  131.9 0.0 copy-start.3
  131.9 6.2 %collective-permute-done.1 = bf16[1536,128]{1,0:T(8,128)(2,1)} collective-permute-done((bf16[1536,128]{1,0:T(8,128)(2,1)S(1)}, bf16[1536,128]{1,0:T(8,128)(2,1)}, u32[]{:S(2)}, u32[]{:S(2)}) %collective-permute-start.1) | collective-permute-done | bytes 393248 | tf_op jit(solution)/shard_map/ppermute | solution.py:23
  138.2 1.1 collective-permute-done.2
  139.3 2.6 %pad_maximum_fusion.1.panel_ref = bf16[1536,512]{1,0:T(8,128)(2,1)} fusion(bf16[1536,128]{1,0:T(8,128)(2,1)} %collective-permute-done.2, bf16[1536,128]{1,0:T(8,128)(2,1)} %collective-permute-done.1, bf16[1536,128]{1,0:T(8,128)(2,1)} %collective-permute-done, bf16[1536,128]{1,0:T(8,128)(2,1)S(1)} %bitcast.11), kind=kLoop, calls=%fused_computation.1 | loop fusion | flops 6291456 | bytes 3145728 | tf_op jit(solution)/shard_map/concatenate | solution.py:124
  141.9 0.0 collective-permute-done.3
  141.9 0.0 collective-permute-done.4
  141.9 6.7 %pad_maximum_fusion.panel_ref = bf16[4096,1024]{1,0:T(8,128)(2,1)} fusion(bf16[4096,256]{1,0:T(8,128)(2,1)} %collective-permute-done.5, bf16[4096,256]{1,0:T(8,128)(2,1)} %collective-permute-done.4, bf16[4096,256]{1,0:T(8,128)(2,1)} %collective-permute-done.3, bf16[4096,256]{1,0:T(8,128)(2,1)S(1)} %bitcast.7), kind=kLoop, calls=%fused_computation | loop fusion | flops 33554432 | bytes 16777216 | tf_op jit(solution)/shard_map/concatenate | solution.py:124
  148.6 6.6 %all-to-all-done.arrived_ref = bf16[128,2,5632]{2,1,0:T(2,128)(2,1)S(1)} async-done(((bf16[128,2,5632]{2,1,0:T(2,128)(2,1)}), bf16[128,2,5632]{2,1,0:T(2,128)(2,1)S(1)}, u32[]{:S(2)}, u32[]{:S(2)}) %all-to-all-start) | async-done | bytes 2883616 | tf_op jit(solution)/shard_map/all_to_all | solution.py:120
  155.3 4.5 %output_squares.1 = bf16[4,256,256]{2,1,0:T(8,128)(2,1)S(1)} custom-call(s32[1]{0:T(128)} %bitcast.me_ref, bf16[128,2,5632]{2,1,0:T(2,128)(2,1)S(1)} %all-to-all-done.arrived_ref, bf16[4096,1024]{1,0:T(8,128)(2,1)} %pad_maximum_fusion.panel_ref), custom_call_target="tpu_custom_call" | custom-call | flops 2147483648 | bytes 8388608 | tf_op jit(solution)/shard_map/output_squares/pallas_call | solution.py:142
  159.8 0.0 copy-start
  159.8 0.8 copy-done
  160.6 4.0 %all-to-all-start.1 = ((bf16[4,256,256]{2,1,0:T(8,128)(2,1)}), bf16[4,256,256]{2,1,0:T(8,128)(2,1)S(1)}, u32[]{:S(2)}, u32[]{:S(2)}) async-start(bf16[4,256,256]{2,1,0:T(8,128)(2,1)} %copy-done), calls=%async_computation.1 | async-start | bytes 1048576 | tf_op jit(solution)/shard_map/all_to_all | solution.py:159
  164.6 1.9 %input_squares.1.refs_0_ = bf16[256,512]{1,0:T(8,128)(2,1)S(1)} custom-call(bf16[128,2,5632]{2,1,0:T(2,128)(2,1)S(1)} %all-to-all-done.arrived_ref, bf16[1536,512]{1,0:T(8,128)(2,1)} %pad_maximum_fusion.1.panel_ref), custom_call_target="tpu_custom_call" | custom-call | tf_op jit(solution)/shard_map/input_squares/pallas_call | solution.py:127
  166.5 4.6 %collective-permute-start.6 = (bf16[256,512]{1,0:T(8,128)(2,1)S(1)}, bf16[256,512]{1,0:T(8,128)(2,1)S(1)}, u32[]{:S(2)}, u32[]{:S(2)}) collective-permute-start(bf16[256,512]{1,0:T(8,128)(2,1)S(1)} %input_squares.1.refs_0_), channel_id=1, source_target_pairs={{0,3},{1,0},{2,1},{3,2},{4,7},{5,4},{6,5},{7,6},{8,11},{9,8},{10,9... | collective-permute-start | bytes 786440 | tf_op jit(solution)/shard_map/ppermute | solution.py:23
  171.1 2.5 %collective-permute-start.7 = (bf16[256,512]{1,0:T(8,128)(2,1)S(1)}, bf16[256,512]{1,0:T(8,128)(2,1)S(1)}, u32[]{:S(2)}, u32[]{:S(2)}) collective-permute-start(bf16[256,512]{1,0:T(8,128)(2,1)S(1)} %input_squares.1.refs_0_), channel_id=1, source_target_pairs={{0,2},{1,3},{2,0},{3,1},{4,6},{5,7},{6,4},{7,5},{8,10},{9,11},{10,... | collective-permute-start | bytes 786440 | tf_op jit(solution)/shard_map/ppermute | solution.py:23
  173.6 2.5 %collective-permute-start.8 = (bf16[256,512]{1,0:T(8,128)(2,1)S(1)}, bf16[256,512]{1,0:T(8,128)(2,1)S(1)}, u32[]{:S(2)}, u32[]{:S(2)}) collective-permute-start(bf16[256,512]{1,0:T(8,128)(2,1)S(1)} %input_squares.1.refs_0_), channel_id=1, source_target_pairs={{0,1},{1,2},{2,3},{3,0},{4,5},{5,6},{6,7},{7,4},{8,9},{9,10},{10,1... | collective-permute-start | bytes 786440 | tf_op jit(solution)/shard_map/ppermute | solution.py:23
  176.1 0.7 copy-done.1
  176.8 0.1 collective-permute-done.6.refs_1_
  176.8 2.9 %collective-permute-done.7.refs_2_ = bf16[256,512]{1,0:T(8,128)(2,1)S(1)} collective-permute-done((bf16[256,512]{1,0:T(8,128)(2,1)S(1)}, bf16[256,512]{1,0:T(8,128)(2,1)S(1)}, u32[]{:S(2)}, u32[]{:S(2)}) %collective-permute-start.7) | collective-permute-done | bytes 262176 | tf_op jit(solution)/shard_map/ppermute | solution.py:23
  179.8 6.5 %collective-permute-done.8.refs_3_ = bf16[256,512]{1,0:T(8,128)(2,1)S(1)} collective-permute-done((bf16[256,512]{1,0:T(8,128)(2,1)S(1)}, bf16[256,512]{1,0:T(8,128)(2,1)S(1)}, u32[]{:S(2)}, u32[]{:S(2)}) %collective-permute-start.8) | collective-permute-done | bytes 262176 | tf_op jit(solution)/shard_map/ppermute | solution.py:23
  186.2 0.9 copy-done.2
  187.2 1.3 tile.1
  (6 shorter events, 0.0 us)
Async XLA Ops:
  4.9 31.3 %copy-start.4 = (bf16[1,1536,128]{2,1,0:T(8,128)(2,1)S(1)}, bf16[1,1536,128]{2,1,0:T(8,128)(2,1)}, u32[]{:S(2)}) copy-start(bf16[1,1536,128]{2,1,0:T(8,128)(2,1)} %param.8) | copy-start | bytes 1179652
  4.9 150.3 %all-to-all-start = ((bf16[128,2,5632]{2,1,0:T(2,128)(2,1)}), bf16[128,2,5632]{2,1,0:T(2,128)(2,1)S(1)}, u32[]{:S(2)}, u32[]{:S(2)}) async-start(bf16[128,2,5632]{2,1,0:T(2,128)(2,1)} %pack.1), calls=%async_computation | async-start | bytes 5767168 | tf_op jit(solution)/shard_map/all_to_all | solution.py:120
  25.6 116.3 %collective-permute-start.3 = (bf16[4096,256]{1,0:T(8,128)(2,1)}, bf16[4096,256]{1,0:T(8,128)(2,1)}, u32[]{:S(2)}, u32[]{:S(2)}) collective-permute-start(bf16[4096,256]{1,0:T(8,128)(2,1)} %bitcast.4), channel_id=1, source_target_pairs={{0,1},{1,2},{2,3},{3,0},{4,5},{5,6},{6,7},{7,4},{8,9},{9,10},{10,1... | collective-permute-start | bytes 6291464 | tf_op jit(solution)/shard_map/ppermute | solution.py:23
  28.8 113.1 %collective-permute-start.4 = (bf16[4096,256]{1,0:T(8,128)(2,1)}, bf16[4096,256]{1,0:T(8,128)(2,1)}, u32[]{:S(2)}, u32[]{:S(2)}) collective-permute-start(bf16[4096,256]{1,0:T(8,128)(2,1)} %bitcast.5), channel_id=1, source_target_pairs={{0,2},{1,3},{2,0},{3,1},{4,6},{5,7},{6,4},{7,5},{8,10},{9,11},{10,... | collective-permute-start | bytes 6291464 | tf_op jit(solution)/shard_map/ppermute | solution.py:23
  33.1 108.8 %collective-permute-start.5 = (bf16[4096,256]{1,0:T(8,128)(2,1)}, bf16[4096,256]{1,0:T(8,128)(2,1)}, u32[]{:S(2)}, u32[]{:S(2)}) collective-permute-start(bf16[4096,256]{1,0:T(8,128)(2,1)} %bitcast.6), channel_id=1, source_target_pairs={{0,3},{1,0},{2,1},{3,2},{4,7},{5,4},{6,5},{7,6},{8,11},{9,8},{10,9... | collective-permute-start | bytes 6291464 | tf_op jit(solution)/shard_map/ppermute | solution.py:23
  36.2 92.5 %collective-permute-start = (bf16[1536,128]{1,0:T(8,128)(2,1)S(1)}, bf16[1536,128]{1,0:T(8,128)(2,1)}, u32[]{:S(2)}, u32[]{:S(2)}) collective-permute-start(bf16[1536,128]{1,0:T(8,128)(2,1)S(1)} %bitcast.8), channel_id=1, source_target_pairs={{0,1},{1,2},{2,3},{3,0},{4,5},{5,6},{6,7},{7,4},{8,9},{9,10},{10,1... | collective-permute-start | bytes 1179656 | tf_op jit(solution)/shard_map/ppermute | solution.py:23
  38.4 99.7 %collective-permute-start.1 = (bf16[1536,128]{1,0:T(8,128)(2,1)S(1)}, bf16[1536,128]{1,0:T(8,128)(2,1)}, u32[]{:S(2)}, u32[]{:S(2)}) collective-permute-start(bf16[1536,128]{1,0:T(8,128)(2,1)S(1)} %bitcast.9), channel_id=1, source_target_pairs={{0,2},{1,3},{2,0},{3,1},{4,6},{5,7},{6,4},{7,5},{8,10},{9,11},{10,... | collective-permute-start | bytes 1179656 | tf_op jit(solution)/shard_map/ppermute | solution.py:23
  128.7 10.6 %collective-permute-start.2 = (bf16[1536,128]{1,0:T(8,128)(2,1)S(1)}, bf16[1536,128]{1,0:T(8,128)(2,1)}, u32[]{:S(2)}, u32[]{:S(2)}) collective-permute-start(bf16[1536,128]{1,0:T(8,128)(2,1)S(1)} %bitcast.10), channel_id=1, source_target_pairs={{0,3},{1,0},{2,1},{3,2},{4,7},{5,4},{6,5},{7,6},{8,11},{9,8},{10,9... | collective-permute-start | bytes 1179656 | tf_op jit(solution)/shard_map/ppermute | solution.py:23
  131.9 10.0 %copy-start.3 = (bf16[1,4096,256]{2,1,0:T(8,128)(2,1)S(1)}, bf16[1,4096,256]{2,1,0:T(8,128)(2,1)}, u32[]{:S(2)}) copy-start(bf16[1,4096,256]{2,1,0:T(8,128)(2,1)} %param.9) | copy-start | bytes 6291460
  159.8 0.8 copy-start
  160.6 25.7 %all-to-all-start.1 = ((bf16[4,256,256]{2,1,0:T(8,128)(2,1)}), bf16[4,256,256]{2,1,0:T(8,128)(2,1)S(1)}, u32[]{:S(2)}, u32[]{:S(2)}) async-start(bf16[4,256,256]{2,1,0:T(8,128)(2,1)} %copy-done), calls=%async_computation.1 | async-start | bytes 1048576 | tf_op jit(solution)/shard_map/all_to_all | solution.py:159
  166.5 10.4 %collective-permute-start.6 = (bf16[256,512]{1,0:T(8,128)(2,1)S(1)}, bf16[256,512]{1,0:T(8,128)(2,1)S(1)}, u32[]{:S(2)}, u32[]{:S(2)}) collective-permute-start(bf16[256,512]{1,0:T(8,128)(2,1)S(1)} %input_squares.1.refs_0_), channel_id=1, source_target_pairs={{0,3},{1,0},{2,1},{3,2},{4,7},{5,4},{6,5},{7,6},{8,11},{9,8},{10,9... | collective-permute-start | bytes 786440 | tf_op jit(solution)/shard_map/ppermute | solution.py:23
  171.1 8.7 %collective-permute-start.7 = (bf16[256,512]{1,0:T(8,128)(2,1)S(1)}, bf16[256,512]{1,0:T(8,128)(2,1)S(1)}, u32[]{:S(2)}, u32[]{:S(2)}) collective-permute-start(bf16[256,512]{1,0:T(8,128)(2,1)S(1)} %input_squares.1.refs_0_), channel_id=1, source_target_pairs={{0,2},{1,3},{2,0},{3,1},{4,6},{5,7},{6,4},{7,5},{8,10},{9,11},{10,... | collective-permute-start | bytes 786440 | tf_op jit(solution)/shard_map/ppermute | solution.py:23
  173.6 12.7 %collective-permute-start.8 = (bf16[256,512]{1,0:T(8,128)(2,1)S(1)}, bf16[256,512]{1,0:T(8,128)(2,1)S(1)}, u32[]{:S(2)}, u32[]{:S(2)}) collective-permute-start(bf16[256,512]{1,0:T(8,128)(2,1)S(1)} %input_squares.1.refs_0_), channel_id=1, source_target_pairs={{0,1},{1,2},{2,3},{3,0},{4,5},{5,6},{6,7},{7,4},{8,9},{9,10},{10,1... | collective-permute-start | bytes 786440 | tf_op jit(solution)/shard_map/ppermute | solution.py:23
  176.1 0.7 copy-start.1
  186.2 1.0 copy-start.2
where the time goes:
time: 192 us; the launch traced here: 188 us
  waiting for transfers between devices  111 us (58%)
  starting transfers between devices  53 us (28%)
  Pallas kernels  12.6 us (7%)
  other arithmetic  9.32 us (5%)
  local copies, waits for them, and re-layouts  2.43 us (1%)
    ppermute x9, waiting for transfers between devices, shifted(): lax.ppermute(values, 'help', [(i, (i + steps) % helpers) for i in range(h...  104 us
    ppermute x9, starting transfers between devices, shifted(): lax.ppermute(values, 'help', [(i, (i + steps) % helpers) for i in range(h...  28.3 us
    all_to_all x1, starting transfers between devices, on_device(): lax.all_to_all(send, 'expert', split_axis=0, concat_axis=0, tiled=True)  20.7 us
    concatenate x1, other arithmetic, on_device(): jnp.concatenate(out_parts, axis=1)  6.73 us
    all_to_all x1, waiting for transfers between devices, on_device(): lax.all_to_all(send, 'expert', split_axis=0, concat_axis=0, tiled=True)  6.62 us
    pallas_call x1, Pallas kernels, on_device(): pl.pallas_call(pack_kernel, out_shape=jax.ShapeDtypeStruct((experts, slot...  4.89 us
    pallas_call x1, Pallas kernels, on_device(): pl.pallas_call(output_kernel, out_shape=jax.ShapeDtypeStruct((helpers, sl...  4.51 us
    all_to_all x1, starting transfers between devices, on_device(): lax.all_to_all(own_out, 'help', split_axis=0, concat_axis=0, tiled=True)  4.01 us
  transfers between devices with their start and end apart: 11, of which 7 were waited for; matrix products, arithmetic and copies ran while one was open for 5% of the time, Pallas kernels for 1%

commit v1 on v0

--- a/solution.py
+++ b/solution.py
@@ -24,13 +24,15 @@
 
 
 def pack_kernel(routing_ref, grad_ref, act_ref, send_ref, rows_ref, packed_ref, in_sems, out_sems):
-    rows, (experts, slots, width) = grad_ref.shape[0], send_ref.shape
-    loads, stores, base = [], [], 0
+    rows, (experts, slots, _) = grad_ref.shape[0], send_ref.shape
+    loads, stores, steps, base = [], [], [], 0
     for ref in (grad_ref, act_ref):
-        for k in range(0, ref.shape[1], CHUNK):
-            at = pl.ds(base + k, CHUNK)
-            loads.append(pltpu.make_async_copy(ref.at[:, pl.ds(k, CHUNK)], rows_ref.at[:, at], in_sems.at[len(loads)]))
+        for k in range(0, ref.shape[1], 2 * CHUNK):
+            size = min(2 * CHUNK, ref.shape[1] - k)
+            at = pl.ds(base + k, size)
+            loads.append(pltpu.make_async_copy(ref.at[:, pl.ds(k, size)], rows_ref.at[:, at], in_sems.at[len(loads)]))
             stores.append(pltpu.make_async_copy(packed_ref.at[:, :, at], send_ref.at[:, :, at], out_sems.at[len(stores)]))
+            steps.append((base + k, size))
         base += ref.shape[1]
     for load in loads:
         load.start()
@@ -40,10 +42,10 @@
     target = routing_ref[...] * slots + jnp.sum(earlier, axis=0, keepdims=True).astype(jnp.int32)
     slot = lax.broadcasted_iota(jnp.int32, (experts * slots, rows), 0)
     pick = jnp.where(slot == target, 1.0, 0.0).astype(jnp.bfloat16)
-    for i, k in enumerate(range(0, width, CHUNK)):
+    for i, (k, size) in enumerate(steps):
         loads[i].wait()
-        taken = jnp.dot(pick, rows_ref[:, k : k + CHUNK], preferred_element_type=jnp.float32)
-        packed_ref[:, :, k : k + CHUNK] = taken.astype(jnp.bfloat16).reshape(experts, slots, CHUNK)
+        taken = jnp.dot(pick, rows_ref[:, k : k + size], preferred_element_type=jnp.float32)
+        packed_ref[:, :, k : k + size] = taken.astype(jnp.bfloat16).reshape(experts, slots, size)
         stores[i].start()
     for store in stores:
         store.wait()
@@ -66,19 +68,24 @@
     return jnp.square(total).astype(jnp.bfloat16)
 
 
-def input_kernel(base, arrived_ref, panel_ref, squares_ref, held_ref, sems):
-    squares_ref[...] = squares_of(arrived_ref, panel_ref, held_ref, sems, base)
+def input_kernel(base, arrived_ref, panel_ref, squares_ref, held_ref, own_ref, sems, out_sems):
+    own_ref[...] = squares_of(arrived_ref, panel_ref, held_ref, sems, base)
+    copies = [pltpu.make_async_copy(own_ref, squares_ref.at[k], out_sems.at[k]) for k in range(squares_ref.shape[0])]
+    for copy in copies:
+        copy.start()
+    for copy in copies:
+        copy.wait()
 
 
-def output_kernel(me_ref, arrived_ref, panel_ref, squares_ref, held_ref, sems):
-    helpers, _, width = squares_ref.shape
+def output_kernel(arrived_ref, panel_ref, *refs):
+    squares_refs, (held_ref, sems) = refs[:-2], refs[-2:]
     squares = squares_of(arrived_ref, panel_ref, held_ref, sems, 0)
-    for k in range(helpers):
-        squares_ref[lax.rem(me_ref[0] + helpers - k, helpers)] = squares[:, k * width : (k + 1) * width]
+    for k, ref in enumerate(squares_refs):
+        ref[...] = squares[:, k * ref.shape[1] : (k + 1) * ref.shape[1]]
 
 
-def tile_kernel(helpers, me_ref, *refs):
-    in_refs, out_ref, tile_ref = refs[:helpers], refs[-2], refs[-1]
+def tile_kernel(helpers, me_ref, in_ref, *refs):
+    out_refs, tile_ref = refs[:-1], refs[-1]
     width = tile_ref.shape[1] // helpers
     me = me_ref[0]
     for j in range(helpers):
@@ -86,8 +93,8 @@
         for k in range(helpers):
             block = (j + k) % helpers
             term = lax.dot_general(
-                in_refs[k][:, block * width : (block + 1) * width],
-                out_ref[lax.rem(me + k, helpers)],
+                in_ref[lax.rem(me + k, helpers), :, block * width : (block + 1) * width],
+                out_refs[k][...],
                 (((0,), (0,)), ((), ())),
                 preferred_element_type=jnp.float32,
             )
@@ -126,24 +133,26 @@
 
     own_in = pl.pallas_call(
         functools.partial(input_kernel, width_out),
-        out_shape=jax.ShapeDtypeStruct((slots * experts, panel_in), jnp.bfloat16),
+        out_shape=pltpu.HBM((helpers, slots * experts, panel_in), jnp.bfloat16),
         in_specs=[VMEM, HBM],
-        out_specs=VMEM,
+        out_specs=HBM,
         scratch_shapes=[
             pltpu.VMEM((width_in, panel_in), jnp.bfloat16),
+            pltpu.VMEM((slots * experts, panel_in), jnp.bfloat16),
             pltpu.SemaphoreType.DMA((width_in // CHUNK,)),
+            pltpu.SemaphoreType.DMA((helpers,)),
         ],
         compiler_params=params(12),
         name="input_squares",
     )(arrived, pltpu.with_memory_space_constraint(joined_in, pltpu.HBM))
-    all_in = [own_in] + [shifted(own_in, helpers - k) for k in range(1, helpers)]
+    all_in = lax.all_to_all(own_in, "help", split_axis=0, concat_axis=0, tiled=True)
 
     me = lax.axis_index("help").astype(jnp.int32)[None]
     own_out = pl.pallas_call(
         output_kernel,
-        out_shape=jax.ShapeDtypeStruct((helpers, slots * experts, part_out), jnp.bfloat16),
-        in_specs=[SMEM, VMEM, HBM],
-        out_specs=VMEM,
+        out_shape=[jax.ShapeDtypeStruct((slots * experts, part_out), jnp.bfloat16)] * helpers,
+        in_specs=[VMEM, HBM],
+        out_specs=[VMEM] * helpers,
         scratch_shapes=[
             pltpu.VMEM((width_out, part_out * helpers), jnp.bfloat16),
             pltpu.SemaphoreType.DMA((width_out // CHUNK,)),
@@ -155,8 +164,8 @@
             transcendentals=0,
         ),
         name="output_squares",
-    )(me, arrived, pltpu.with_memory_space_constraint(joined_out, pltpu.HBM))
-    all_out = lax.all_to_all(own_out, "help", split_axis=0, concat_axis=0, tiled=True)
+    )(arrived, pltpu.with_memory_space_constraint(joined_out, pltpu.HBM))
+    all_out = [own_out[0]] + [shifted(own_out[k], helpers - k) for k in range(1, helpers)]
 
     return pl.pallas_call(
         functools.partial(tile_kernel, helpers),
@@ -165,7 +174,7 @@
         out_specs=VMEM,
         compiler_params=params(12),
         name="tile",
-    )(me, *all_in, all_out)
+    )(me, all_in, *all_out)
 
 
 def solution(mesh):

time: 192 us -> 187 us (0.974)
  other arithmetic: 9.32 us -> 5.27 us
  local copies, waits for them, and re-layouts: 2.43 us -> 0.01 us
    ppermute x9, waiting for transfers between devices: 104 us -> 99.4 us  [shifted(): lax.ppermute(values, 'help', [(i, (i + steps) % helpers) for i in range(h...]
    all_to_all x1, waiting for transfers between devices: 6.62 us -> 10.7 us  [on_device(): lax.all_to_all(send, 'expert', split_axis=0, concat_axis=0, tiled=True)]
    concatenate x1, other arithmetic: 6.73 us -> 3.91 us  [on_device(): jnp.concatenate(out_parts, axis=1)]
    unnamed x10 -> x4, local copies, waits for them, and re-layouts: 2.43 us -> 0.01 us
  transfers between devices with their start and end apart: 11 -> 11, of which waited for: 7 -> 6; matrix products, arithmetic and copies ran while one was open for 5% -> 3% of each run, Pallas kernels for 1% -> 2%
where the time goes in v1:
time: 187 us; the launch traced here: 183 us
  waiting for transfers between devices  110 us (59%)
  starting transfers between devices  53.4 us (29%)
  Pallas kernels  14.2 us (8%)
  other arithmetic  5.27 us (3%)
    ppermute x9, waiting for transfers between devices, shifted(): lax.ppermute(values, 'help', [(i, (i + steps) % helpers) for i in range(h...  99.4 us
    ppermute x9, starting transfers between devices, shifted(): lax.ppermute(values, 'help', [(i, (i + steps) % helpers) for i in range(h...  28.4 us
    all_to_all x1, starting transfers between devices, on_device(): lax.all_to_all(send, 'expert', split_axis=0, concat_axis=0, tiled=True)  20.7 us
    all_to_all x1, waiting for transfers between devices, on_device(): lax.all_to_all(send, 'expert', split_axis=0, concat_axis=0, tiled=True)  10.7 us
    pallas_call x1, Pallas kernels, on_device(): pl.pallas_call(output_kernel, out_shape=[jax.ShapeDtypeStruct((slots * ex...  4.51 us
    all_to_all x1, starting transfers between devices, on_device(): lax.all_to_all(own_in, 'help', split_axis=0, concat_axis=0, tiled=True)  4.27 us
    pallas_call x1, Pallas kernels, on_device(): pl.pallas_call(pack_kernel, out_shape=jax.ShapeDtypeStruct((experts, slot...  4.22 us
    concatenate x1, other arithmetic, on_device(): jnp.concatenate(out_parts, axis=1)  3.91 us
  transfers between devices with their start and end apart: 11, of which 6 were waited for; matrix products, arithmetic and copies ran while one was open for 3% of the time, Pallas kernels for 2%

profile of v1, /device:TPU:1, one launch (start us, length us, event | category | flops | bytes accessed | tf_op | source)
XLA Modules:
  0.0 183.1 jit_solution(16801103171506156264)
XLA Ops:
  0.0 4.2 %pack.1 = bf16[128,2,5632]{2,1,0:T(2,128)(2,1)} custom-call(s32[1,128]{1,0:T(1,128)} %bitcast.12, bf16[128,4096]{1,0:T(8,128)(2,1)} %grad_ref.1, bf16[128,1536]{1,0:T(8,128)(2,1)} %act_ref.1), custom_call_target="tpu_custom_call" | custom-call | tf_op jit(solution)/shard_map/pack/pallas_call | solution.py:113
  4.2 0.0 copy-start.1
  4.2 20.7 %all-to-all-start = ((bf16[128,2,5632]{2,1,0:T(2,128)(2,1)}), bf16[128,2,5632]{2,1,0:T(2,128)(2,1)S(1)}, u32[]{:S(2)}, u32[]{:S(2)}) async-start(bf16[128,2,5632]{2,1,0:T(2,128)(2,1)} %pack.1), calls=%async_computation | async-start | bytes 5767168 | tf_op jit(solution)/shard_map/all_to_all | solution.py:127
  24.9 0.0 copy-start
  25.0 3.3 %collective-permute-start.3 = (bf16[4096,256]{1,0:T(8,128)(2,1)}, bf16[4096,256]{1,0:T(8,128)(2,1)S(1)}, u32[]{:S(2)}, u32[]{:S(2)}) collective-permute-start(bf16[4096,256]{1,0:T(8,128)(2,1)} %bitcast.4), channel_id=1, source_target_pairs={{0,1},{1,2},{2,3},{3,0},{4,5},{5,6},{6,7},{7,4},{8,9},{9,10},{10,1... | collective-permute-start | bytes 6291464 | tf_op jit(solution)/shard_map/ppermute | solution.py:23
  28.2 4.4 %collective-permute-start.4 = (bf16[4096,256]{1,0:T(8,128)(2,1)}, bf16[4096,256]{1,0:T(8,128)(2,1)S(1)}, u32[]{:S(2)}, u32[]{:S(2)}) collective-permute-start(bf16[4096,256]{1,0:T(8,128)(2,1)} %bitcast.5), channel_id=1, source_target_pairs={{0,2},{1,3},{2,0},{3,1},{4,6},{5,7},{6,4},{7,5},{8,10},{9,11},{10,... | collective-permute-start | bytes 6291464 | tf_op jit(solution)/shard_map/ppermute | solution.py:23
  32.6 3.1 %collective-permute-start.5 = (bf16[4096,256]{1,0:T(8,128)(2,1)}, bf16[4096,256]{1,0:T(8,128)(2,1)S(1)}, u32[]{:S(2)}, u32[]{:S(2)}) collective-permute-start(bf16[4096,256]{1,0:T(8,128)(2,1)} %bitcast.6), channel_id=1, source_target_pairs={{0,3},{1,0},{2,1},{3,2},{4,7},{5,4},{6,5},{7,6},{8,11},{9,8},{10,9... | collective-permute-start | bytes 6291464 | tf_op jit(solution)/shard_map/ppermute | solution.py:23
  35.7 0.0 copy-done.1
  35.7 2.2 %collective-permute-start = (bf16[1536,128]{1,0:T(8,128)(2,1)S(1)}, bf16[1536,128]{1,0:T(8,128)(2,1)S(1)}, u32[]{:S(2)}, u32[]{:S(2)}) collective-permute-start(bf16[1536,128]{1,0:T(8,128)(2,1)S(1)} %bitcast.8), channel_id=1, source_target_pairs={{0,1},{1,2},{2,3},{3,0},{4,5},{5,6},{6,7},{7,4},{8,9},{9,10},{10,1... | collective-permute-start | bytes 1179656 | tf_op jit(solution)/shard_map/ppermute | solution.py:23
  37.9 2.8 %collective-permute-start.1 = (bf16[1536,128]{1,0:T(8,128)(2,1)S(1)}, bf16[1536,128]{1,0:T(8,128)(2,1)S(1)}, u32[]{:S(2)}, u32[]{:S(2)}) collective-permute-start(bf16[1536,128]{1,0:T(8,128)(2,1)S(1)} %bitcast.9), channel_id=1, source_target_pairs={{0,2},{1,3},{2,0},{3,1},{4,6},{5,7},{6,4},{7,5},{8,10},{9,11},{10,... | collective-permute-start | bytes 1179656 | tf_op jit(solution)/shard_map/ppermute | solution.py:23
  40.7 87.4 %collective-permute-done = bf16[1536,128]{1,0:T(8,128)(2,1)S(1)} collective-permute-done((bf16[1536,128]{1,0:T(8,128)(2,1)S(1)}, bf16[1536,128]{1,0:T(8,128)(2,1)S(1)}, u32[]{:S(2)}, u32[]{:S(2)}) %collective-permute-start) | collective-permute-done | bytes 393248 | tf_op jit(solution)/shard_map/ppermute | solution.py:23
  128.1 3.2 %collective-permute-start.2 = (bf16[1536,128]{1,0:T(8,128)(2,1)S(1)}, bf16[1536,128]{1,0:T(8,128)(2,1)S(1)}, u32[]{:S(2)}, u32[]{:S(2)}) collective-permute-start(bf16[1536,128]{1,0:T(8,128)(2,1)S(1)} %bitcast.10), channel_id=1, source_target_pairs={{0,3},{1,0},{2,1},{3,2},{4,7},{5,4},{6,5},{7,6},{8,11},{9,8},{10,9... | collective-permute-start | bytes 1179656 | tf_op jit(solution)/shard_map/ppermute | solution.py:23
  131.3 6.2 %collective-permute-done.1 = bf16[1536,128]{1,0:T(8,128)(2,1)S(1)} collective-permute-done((bf16[1536,128]{1,0:T(8,128)(2,1)S(1)}, bf16[1536,128]{1,0:T(8,128)(2,1)S(1)}, u32[]{:S(2)}, u32[]{:S(2)}) %collective-permute-start.1) | collective-permute-done | bytes 393248 | tf_op jit(solution)/shard_map/ppermute | solution.py:23
  137.5 1.0 collective-permute-done.2
  138.6 1.4 pad_maximum_fusion.1.panel_ref
  139.9 0.0 collective-permute-done.3
  139.9 0.0 collective-permute-done.4
  139.9 0.0 collective-permute-done.5
  139.9 0.0 copy-done
  139.9 3.9 %pad_maximum_fusion.panel_ref = bf16[4096,1024]{1,0:T(8,128)(2,1)} fusion(bf16[4096,256]{1,0:T(8,128)(2,1)S(1)} %collective-permute-done.5, bf16[4096,256]{1,0:T(8,128)(2,1)S(1)} %collective-permute-done.4, bf16[4096,256]{1,0:T(8,128)(2,1)S(1)} %collective-permute-done.3, bf16[4096,256]{1,0:T(8,128)(2,1)S(1)} %bitcast.7), kind=kLoop, calls=%fused_computation | loop fusion | flops 33554432 | bytes 16777216 | tf_op jit(solution)/shard_map/concatenate | solution.py:131
  143.8 10.7 %all-to-all-done.arrived_ref = bf16[128,2,5632]{2,1,0:T(2,128)(2,1)S(1)} async-done(((bf16[128,2,5632]{2,1,0:T(2,128)(2,1)}), bf16[128,2,5632]{2,1,0:T(2,128)(2,1)S(1)}, u32[]{:S(2)}, u32[]{:S(2)}) %all-to-all-start) | async-done | bytes 2883616 | tf_op jit(solution)/shard_map/all_to_all | solution.py:127
  154.6 3.0 %input_squares.1 = bf16[4,256,512]{2,1,0:T(8,128)(2,1)} custom-call(bf16[128,2,5632]{2,1,0:T(2,128)(2,1)S(1)} %all-to-all-done.arrived_ref, bf16[1536,512]{1,0:T(8,128)(2,1)} %pad_maximum_fusion.1.panel_ref), custom_call_target="tpu_custom_call" | custom-call | tf_op jit(solution)/shard_map/input_squares/pallas_call | solution.py:134
  157.6 4.3 %all-to-all-start.1 = ((bf16[4,256,512]{2,1,0:T(8,128)(2,1)}), bf16[4,256,512]{2,1,0:T(8,128)(2,1)}, u32[]{:S(2)}, u32[]{:S(2)}) async-start(bf16[4,256,512]{2,1,0:T(8,128)(2,1)} %input_squares.1), calls=%async_computation.1 | async-start | bytes 2097152 | tf_op jit(solution)/shard_map/all_to_all | solution.py:148
  161.9 4.5 %output_squares.1 = (bf16[256,256]{1,0:T(8,128)(2,1)S(1)}, bf16[256,256]{1,0:T(8,128)(2,1)S(1)}, bf16[256,256]{1,0:T(8,128)(2,1)S(1)}, bf16[256,256]{1,0:T(8,128)(2,1)S(1)}) custom-call(bf16[128,2,5632]{2,1,0:T(2,128)(2,1)S(1)} %all-to-all-done.arrived_ref, bf16[4096,1024]{1,0:T(8,128)(2,1)} %pad_maximum_fusion.panel_ref), custom_call_target="tpu_custom_call" | custom-call | flops 2147483648 | bytes 8388608 | tf_op jit(solution)/shard_map/output_squares/pallas_call | solution.py:151
  166.4 4.5 %collective-permute-start.6 = (bf16[256,256]{1,0:T(8,128)(2,1)S(1)}, bf16[256,256]{1,0:T(8,128)(2,1)S(1)}, u32[]{:S(2)}, u32[]{:S(2)}) collective-permute-start(bf16[256,256]{1,0:T(8,128)(2,1)S(1)} %get-tuple-element.16), channel_id=1, source_target_pairs={{0,3},{1,0},{2,1},{3,2},{4,7},{5,4},{6,5},{7,6},{8,11},{9,8},{10,9... | collective-permute-start | bytes 393224 | tf_op jit(solution)/shard_map/ppermute | solution.py:23
  170.9 2.5 %collective-permute-start.7 = (bf16[256,256]{1,0:T(8,128)(2,1)S(1)}, bf16[256,256]{1,0:T(8,128)(2,1)S(1)}, u32[]{:S(2)}, u32[]{:S(2)}) collective-permute-start(bf16[256,256]{1,0:T(8,128)(2,1)S(1)} %get-tuple-element.17), channel_id=1, source_target_pairs={{0,2},{1,3},{2,0},{3,1},{4,6},{5,7},{6,4},{7,5},{8,10},{9,11},{10,... | collective-permute-start | bytes 393224 | tf_op jit(solution)/shard_map/ppermute | solution.py:23
  173.4 2.5 %collective-permute-start.8 = (bf16[256,256]{1,0:T(8,128)(2,1)S(1)}, bf16[256,256]{1,0:T(8,128)(2,1)S(1)}, u32[]{:S(2)}, u32[]{:S(2)}) collective-permute-start(bf16[256,256]{1,0:T(8,128)(2,1)S(1)} %get-tuple-element.18), channel_id=1, source_target_pairs={{0,1},{1,2},{2,3},{3,0},{4,5},{5,6},{6,7},{7,4},{8,9},{9,10},{10,1... | collective-permute-start | bytes 393224 | tf_op jit(solution)/shard_map/ppermute | solution.py:23
  175.9 0.0 collective-permute-done.6.refs_1_
  175.9 2.7 %collective-permute-done.7.refs_2_ = bf16[256,256]{1,0:T(8,128)(2,1)S(1)} collective-permute-done((bf16[256,256]{1,0:T(8,128)(2,1)S(1)}, bf16[256,256]{1,0:T(8,128)(2,1)S(1)}, u32[]{:S(2)}, u32[]{:S(2)}) %collective-permute-start.7) | collective-permute-done | bytes 131104 | tf_op jit(solution)/shard_map/ppermute | solution.py:23
  178.6 2.1 %collective-permute-done.8.refs_3_ = bf16[256,256]{1,0:T(8,128)(2,1)S(1)} collective-permute-done((bf16[256,256]{1,0:T(8,128)(2,1)S(1)}, bf16[256,256]{1,0:T(8,128)(2,1)S(1)}, u32[]{:S(2)}, u32[]{:S(2)}) %collective-permute-start.8) | collective-permute-done | bytes 131104 | tf_op jit(solution)/shard_map/ppermute | solution.py:23
  180.6 0.0 all-to-all-done.1.in_ref
  180.6 2.5 %tile.1 = f32[1,512,256]{2,1,0:T(8,128)} custom-call(s32[1]{0:T(128)} %bitcast.me_ref, bf16[4,256,512]{2,1,0:T(8,128)(2,1)} %all-to-all-done.1.in_ref, bf16[256,256]{1,0:T(8,128)(2,1)S(1)} %get-tuple-element.15.refs_0_, bf16[256,256]{1,0:T(8,128)(2,1)S(1)} %collective-permute-done.6.refs_1_, bf16[256,256]{1,0:T(8,128)(2,1)S(1)} %collective-permute-done.7.refs_2_, ...), custom_call_target="tpu_custom_call" | custom-call | tf_op jit(solution)/shard_map/tile/pallas_call | solution.py:170
Async XLA Ops:
  4.2 31.4 %copy-start.1 = (bf16[1,1536,128]{2,1,0:T(8,128)(2,1)S(1)}, bf16[1,1536,128]{2,1,0:T(8,128)(2,1)}, u32[]{:S(2)}) copy-start(bf16[1,1536,128]{2,1,0:T(8,128)(2,1)} %param.8) | copy-start | bytes 1179652
  4.2 150.3 %all-to-all-start = ((bf16[128,2,5632]{2,1,0:T(2,128)(2,1)}), bf16[128,2,5632]{2,1,0:T(2,128)(2,1)S(1)}, u32[]{:S(2)}, u32[]{:S(2)}) async-start(bf16[128,2,5632]{2,1,0:T(2,128)(2,1)} %pack.1), calls=%async_computation | async-start | bytes 5767168 | tf_op jit(solution)/shard_map/all_to_all | solution.py:127
  24.9 115.0 %copy-start = (bf16[1,4096,256]{2,1,0:T(8,128)(2,1)S(1)}, bf16[1,4096,256]{2,1,0:T(8,128)(2,1)}, u32[]{:S(2)}) copy-start(bf16[1,4096,256]{2,1,0:T(8,128)(2,1)} %param.9) | copy-start | bytes 6291460
  25.0 115.0 %collective-permute-start.3 = (bf16[4096,256]{1,0:T(8,128)(2,1)}, bf16[4096,256]{1,0:T(8,128)(2,1)S(1)}, u32[]{:S(2)}, u32[]{:S(2)}) collective-permute-start(bf16[4096,256]{1,0:T(8,128)(2,1)} %bitcast.4), channel_id=1, source_target_pairs={{0,1},{1,2},{2,3},{3,0},{4,5},{5,6},{6,7},{7,4},{8,9},{9,10},{10,1... | collective-permute-start | bytes 6291464 | tf_op jit(solution)/shard_map/ppermute | solution.py:23
  28.2 111.7 %collective-permute-start.4 = (bf16[4096,256]{1,0:T(8,128)(2,1)}, bf16[4096,256]{1,0:T(8,128)(2,1)S(1)}, u32[]{:S(2)}, u32[]{:S(2)}) collective-permute-start(bf16[4096,256]{1,0:T(8,128)(2,1)} %bitcast.5), channel_id=1, source_target_pairs={{0,2},{1,3},{2,0},{3,1},{4,6},{5,7},{6,4},{7,5},{8,10},{9,11},{10,... | collective-permute-start | bytes 6291464 | tf_op jit(solution)/shard_map/ppermute | solution.py:23
  32.6 107.3 %collective-permute-start.5 = (bf16[4096,256]{1,0:T(8,128)(2,1)}, bf16[4096,256]{1,0:T(8,128)(2,1)S(1)}, u32[]{:S(2)}, u32[]{:S(2)}) collective-permute-start(bf16[4096,256]{1,0:T(8,128)(2,1)} %bitcast.6), channel_id=1, source_target_pairs={{0,3},{1,0},{2,1},{3,2},{4,7},{5,4},{6,5},{7,6},{8,11},{9,8},{10,9... | collective-permute-start | bytes 6291464 | tf_op jit(solution)/shard_map/ppermute | solution.py:23
  35.7 92.4 %collective-permute-start = (bf16[1536,128]{1,0:T(8,128)(2,1)S(1)}, bf16[1536,128]{1,0:T(8,128)(2,1)S(1)}, u32[]{:S(2)}, u32[]{:S(2)}) collective-permute-start(bf16[1536,128]{1,0:T(8,128)(2,1)S(1)} %bitcast.8), channel_id=1, source_target_pairs={{0,1},{1,2},{2,3},{3,0},{4,5},{5,6},{6,7},{7,4},{8,9},{9,10},{10,1... | collective-permute-start | bytes 1179656 | tf_op jit(solution)/shard_map/ppermute | solution.py:23
  37.9 99.6 %collective-permute-start.1 = (bf16[1536,128]{1,0:T(8,128)(2,1)S(1)}, bf16[1536,128]{1,0:T(8,128)(2,1)S(1)}, u32[]{:S(2)}, u32[]{:S(2)}) collective-permute-start(bf16[1536,128]{1,0:T(8,128)(2,1)S(1)} %bitcast.9), channel_id=1, source_target_pairs={{0,2},{1,3},{2,0},{3,1},{4,6},{5,7},{6,4},{7,5},{8,10},{9,11},{10,... | collective-permute-start | bytes 1179656 | tf_op jit(solution)/shard_map/ppermute | solution.py:23
  128.1 10.5 %collective-permute-start.2 = (bf16[1536,128]{1,0:T(8,128)(2,1)S(1)}, bf16[1536,128]{1,0:T(8,128)(2,1)S(1)}, u32[]{:S(2)}, u32[]{:S(2)}) collective-permute-start(bf16[1536,128]{1,0:T(8,128)(2,1)S(1)} %bitcast.10), channel_id=1, source_target_pairs={{0,3},{1,0},{2,1},{3,2},{4,7},{5,4},{6,5},{7,6},{8,11},{9,8},{10,9... | collective-permute-start | bytes 1179656 | tf_op jit(solution)/shard_map/ppermute | solution.py:23
  157.6 23.1 %all-to-all-start.1 = ((bf16[4,256,512]{2,1,0:T(8,128)(2,1)}), bf16[4,256,512]{2,1,0:T(8,128)(2,1)}, u32[]{:S(2)}, u32[]{:S(2)}) async-start(bf16[4,256,512]{2,1,0:T(8,128)(2,1)} %input_squares.1), calls=%async_computation.1 | async-start | bytes 2097152 | tf_op jit(solution)/shard_map/all_to_all | solution.py:148
  166.4 9.5 %collective-permute-start.6 = (bf16[256,256]{1,0:T(8,128)(2,1)S(1)}, bf16[256,256]{1,0:T(8,128)(2,1)S(1)}, u32[]{:S(2)}, u32[]{:S(2)}) collective-permute-start(bf16[256,256]{1,0:T(8,128)(2,1)S(1)} %get-tuple-element.16), channel_id=1, source_target_pairs={{0,3},{1,0},{2,1},{3,2},{4,7},{5,4},{6,5},{7,6},{8,11},{9,8},{10,9... | collective-permute-start | bytes 393224 | tf_op jit(solution)/shard_map/ppermute | solution.py:23
  170.9 7.7 %collective-permute-start.7 = (bf16[256,256]{1,0:T(8,128)(2,1)S(1)}, bf16[256,256]{1,0:T(8,128)(2,1)S(1)}, u32[]{:S(2)}, u32[]{:S(2)}) collective-permute-start(bf16[256,256]{1,0:T(8,128)(2,1)S(1)} %get-tuple-element.17), channel_id=1, source_target_pairs={{0,2},{1,3},{2,0},{3,1},{4,6},{5,7},{6,4},{7,5},{8,10},{9,11},{10,... | collective-permute-start | bytes 393224 | tf_op jit(solution)/shard_map/ppermute | solution.py:23
  173.4 7.2 %collective-permute-start.8 = (bf16[256,256]{1,0:T(8,128)(2,1)S(1)}, bf16[256,256]{1,0:T(8,128)(2,1)S(1)}, u32[]{:S(2)}, u32[]{:S(2)}) collective-permute-start(bf16[256,256]{1,0:T(8,128)(2,1)S(1)} %get-tuple-element.18), channel_id=1, source_target_pairs={{0,1},{1,2},{2,3},{3,0},{4,5},{5,6},{6,7},{7,4},{8,9},{9,10},{10,1... | collective-permute-start | bytes 393224 | tf_op jit(solution)/shard_map/ppermute | solution.py:23

commit v2 on v1

--- a/solution.py
+++ b/solution.py
@@ -85,22 +85,29 @@
 
 
 def tile_kernel(helpers, me_ref, in_ref, *refs):
-    out_refs, tile_ref = refs[:-1], refs[-1]
+    out_refs, (tile_ref, held_ref, sems) = refs[:helpers], refs[helpers:]
     width = tile_ref.shape[1] // helpers
     me = me_ref[0]
-    for j in range(helpers):
-        total = None
-        for k in range(helpers):
+    loads = [
+        pltpu.make_async_copy(in_ref.at[lax.rem(me + k, helpers)], held_ref.at[k], sems.at[k]) for k in range(helpers)
+    ]
+    for load in loads:
+        load.start()
+    totals = [None] * helpers
+    for k in range(helpers):
+        loads[k].wait()
+        for j in range(helpers):
             block = (j + k) % helpers
             term = lax.dot_general(
-                in_ref[lax.rem(me + k, helpers), :, block * width : (block + 1) * width],
+                held_ref[k, :, block * width : (block + 1) * width],
                 out_refs[k][...],
                 (((0,), (0,)), ((), ())),
                 preferred_element_type=jnp.float32,
             )
-            total = term if total is None else total + term
+            totals[j] = term if totals[j] is None else totals[j] + term
+    for j in range(helpers):
         start = pl.multiple_of(lax.rem(me + helpers - j, helpers) * width, width)
-        tile_ref[0, pl.ds(start, width), :] = total
+        tile_ref[0, pl.ds(start, width), :] = totals[j]
 
 
 def on_device(act_rows, grad_rows, routing, input_panel, output_panel):
@@ -165,16 +172,22 @@
         ),
         name="output_squares",
     )(arrived, pltpu.with_memory_space_constraint(joined_out, pltpu.HBM))
-    all_out = [own_out[0]] + [shifted(own_out[k], helpers - k) for k in range(1, helpers)]
+    all_out = [own_out[0]]
+    for k in range(1, helpers):
+        all_out.append(shifted(own_out[k], helpers - k))
 
     return pl.pallas_call(
         functools.partial(tile_kernel, helpers),
         out_shape=jax.ShapeDtypeStruct((1, panel_in, part_out), jnp.float32),
-        in_specs=[SMEM] + [VMEM] * (helpers + 1),
+        in_specs=[SMEM, HBM] + [VMEM] * helpers,
         out_specs=VMEM,
+        scratch_shapes=[
+            pltpu.VMEM((helpers, slots * experts, panel_in), jnp.bfloat16),
+            pltpu.SemaphoreType.DMA((helpers,)),
+        ],
         compiler_params=params(12),
         name="tile",
-    )(me, all_in, *all_out)
+    )(me, pltpu.with_memory_space_constraint(all_in, pltpu.HBM), *all_out)
 
 
 def solution(mesh):

time: 187 us -> 187 us (level)
  no operation moved by 1% of the time
where the time goes in v2:
time: 187 us; the launch traced here: 183 us
  waiting for transfers between devices  110 us (59%)
  starting transfers between devices  53.4 us (29%)
  Pallas kernels  14.2 us (8%)
  other arithmetic  5.27 us (3%)
    ppermute x9, waiting for transfers between devices, shifted(): lax.ppermute(values, 'help', [(i, (i + steps) % helpers) for i in range(h...  99.4 us
    ppermute x9, starting transfers between devices, shifted(): lax.ppermute(values, 'help', [(i, (i + steps) % helpers) for i in range(h...  28.4 us
    all_to_all x1, starting transfers between devices, on_device(): lax.all_to_all(send, 'expert', split_axis=0, concat_axis=0, tiled=True)  20.7 us
    all_to_all x1, waiting for transfers between devices, on_device(): lax.all_to_all(send, 'expert', split_axis=0, concat_axis=0, tiled=True)  10.7 us
    pallas_call x1, Pallas kernels, on_device(): pl.pallas_call(output_kernel, out_shape=[jax.ShapeDtypeStruct((slots * ex...  4.51 us
    all_to_all x1, starting transfers between devices, on_device(): lax.all_to_all(own_in, 'help', split_axis=0, concat_axis=0, tiled=True)  4.27 us
    pallas_call x1, Pallas kernels, on_device(): pl.pallas_call(pack_kernel, out_shape=jax.ShapeDtypeStruct((experts, slot...  4.22 us
    concatenate x1, other arithmetic, on_device(): jnp.concatenate(out_parts, axis=1)  3.91 us
  transfers between devices with their start and end apart: 11, of which 6 were waited for; matrix products, arithmetic and copies ran while one was open for 3% of the time, Pallas kernels for 2%

profile of v2, /device:TPU:1, one launch (start us, length us, event | category | flops | bytes accessed | tf_op | source)
XLA Modules:
  0.0 183.2 jit_solution(6009777261619468082)
XLA Ops:
  0.0 4.2 %pack.1 = bf16[128,2,5632]{2,1,0:T(2,128)(2,1)} custom-call(s32[1,128]{1,0:T(1,128)} %bitcast.12, bf16[128,4096]{1,0:T(8,128)(2,1)} %grad_ref.1, bf16[128,1536]{1,0:T(8,128)(2,1)} %act_ref.1), custom_call_target="tpu_custom_call" | custom-call | tf_op jit(solution)/shard_map/pack/pallas_call | solution.py:120
  4.2 0.0 copy-start.1
  4.2 20.7 %all-to-all-start = ((bf16[128,2,5632]{2,1,0:T(2,128)(2,1)}), bf16[128,2,5632]{2,1,0:T(2,128)(2,1)S(1)}, u32[]{:S(2)}, u32[]{:S(2)}) async-start(bf16[128,2,5632]{2,1,0:T(2,128)(2,1)} %pack.1), calls=%async_computation | async-start | bytes 5767168 | tf_op jit(solution)/shard_map/all_to_all | solution.py:134
  24.9 0.0 copy-start
  25.0 3.3 %collective-permute-start.3 = (bf16[4096,256]{1,0:T(8,128)(2,1)}, bf16[4096,256]{1,0:T(8,128)(2,1)S(1)}, u32[]{:S(2)}, u32[]{:S(2)}) collective-permute-start(bf16[4096,256]{1,0:T(8,128)(2,1)} %bitcast.4), channel_id=1, source_target_pairs={{0,1},{1,2},{2,3},{3,0},{4,5},{5,6},{6,7},{7,4},{8,9},{9,10},{10,1... | collective-permute-start | bytes 6291464 | tf_op jit(solution)/shard_map/ppermute | solution.py:23
  28.2 4.4 %collective-permute-start.4 = (bf16[4096,256]{1,0:T(8,128)(2,1)}, bf16[4096,256]{1,0:T(8,128)(2,1)S(1)}, u32[]{:S(2)}, u32[]{:S(2)}) collective-permute-start(bf16[4096,256]{1,0:T(8,128)(2,1)} %bitcast.5), channel_id=1, source_target_pairs={{0,2},{1,3},{2,0},{3,1},{4,6},{5,7},{6,4},{7,5},{8,10},{9,11},{10,... | collective-permute-start | bytes 6291464 | tf_op jit(solution)/shard_map/ppermute | solution.py:23
  32.6 3.1 %collective-permute-start.5 = (bf16[4096,256]{1,0:T(8,128)(2,1)}, bf16[4096,256]{1,0:T(8,128)(2,1)S(1)}, u32[]{:S(2)}, u32[]{:S(2)}) collective-permute-start(bf16[4096,256]{1,0:T(8,128)(2,1)} %bitcast.6), channel_id=1, source_target_pairs={{0,3},{1,0},{2,1},{3,2},{4,7},{5,4},{6,5},{7,6},{8,11},{9,8},{10,9... | collective-permute-start | bytes 6291464 | tf_op jit(solution)/shard_map/ppermute | solution.py:23
  35.7 0.0 copy-done.1
  35.7 2.2 %collective-permute-start = (bf16[1536,128]{1,0:T(8,128)(2,1)S(1)}, bf16[1536,128]{1,0:T(8,128)(2,1)S(1)}, u32[]{:S(2)}, u32[]{:S(2)}) collective-permute-start(bf16[1536,128]{1,0:T(8,128)(2,1)S(1)} %bitcast.8), channel_id=1, source_target_pairs={{0,1},{1,2},{2,3},{3,0},{4,5},{5,6},{6,7},{7,4},{8,9},{9,10},{10,1... | collective-permute-start | bytes 1179656 | tf_op jit(solution)/shard_map/ppermute | solution.py:23
  37.9 2.8 %collective-permute-start.1 = (bf16[1536,128]{1,0:T(8,128)(2,1)S(1)}, bf16[1536,128]{1,0:T(8,128)(2,1)S(1)}, u32[]{:S(2)}, u32[]{:S(2)}) collective-permute-start(bf16[1536,128]{1,0:T(8,128)(2,1)S(1)} %bitcast.9), channel_id=1, source_target_pairs={{0,2},{1,3},{2,0},{3,1},{4,6},{5,7},{6,4},{7,5},{8,10},{9,11},{10,... | collective-permute-start | bytes 1179656 | tf_op jit(solution)/shard_map/ppermute | solution.py:23
  40.7 87.4 %collective-permute-done = bf16[1536,128]{1,0:T(8,128)(2,1)S(1)} collective-permute-done((bf16[1536,128]{1,0:T(8,128)(2,1)S(1)}, bf16[1536,128]{1,0:T(8,128)(2,1)S(1)}, u32[]{:S(2)}, u32[]{:S(2)}) %collective-permute-start) | collective-permute-done | bytes 393248 | tf_op jit(solution)/shard_map/ppermute | solution.py:23
  128.1 3.2 %collective-permute-start.2 = (bf16[1536,128]{1,0:T(8,128)(2,1)S(1)}, bf16[1536,128]{1,0:T(8,128)(2,1)S(1)}, u32[]{:S(2)}, u32[]{:S(2)}) collective-permute-start(bf16[1536,128]{1,0:T(8,128)(2,1)S(1)} %bitcast.10), channel_id=1, source_target_pairs={{0,3},{1,0},{2,1},{3,2},{4,7},{5,4},{6,5},{7,6},{8,11},{9,8},{10,9... | collective-permute-start | bytes 1179656 | tf_op jit(solution)/shard_map/ppermute | solution.py:23
  131.3 6.2 %collective-permute-done.1 = bf16[1536,128]{1,0:T(8,128)(2,1)S(1)} collective-permute-done((bf16[1536,128]{1,0:T(8,128)(2,1)S(1)}, bf16[1536,128]{1,0:T(8,128)(2,1)S(1)}, u32[]{:S(2)}, u32[]{:S(2)}) %collective-permute-start.1) | collective-permute-done | bytes 393248 | tf_op jit(solution)/shard_map/ppermute | solution.py:23
  137.5 1.0 collective-permute-done.2
  138.6 1.4 pad_maximum_fusion.1.panel_ref
  139.9 0.0 collective-permute-done.3
  139.9 0.0 collective-permute-done.4
  139.9 0.0 collective-permute-done.5
  139.9 0.0 copy-done
  139.9 3.9 %pad_maximum_fusion.panel_ref = bf16[4096,1024]{1,0:T(8,128)(2,1)} fusion(bf16[4096,256]{1,0:T(8,128)(2,1)S(1)} %collective-permute-done.5, bf16[4096,256]{1,0:T(8,128)(2,1)S(1)} %collective-permute-done.4, bf16[4096,256]{1,0:T(8,128)(2,1)S(1)} %collective-permute-done.3, bf16[4096,256]{1,0:T(8,128)(2,1)S(1)} %bitcast.7), kind=kLoop, calls=%fused_computation | loop fusion | flops 33554432 | bytes 16777216 | tf_op jit(solution)/shard_map/concatenate | solution.py:138
  143.8 10.7 %all-to-all-done.arrived_ref = bf16[128,2,5632]{2,1,0:T(2,128)(2,1)S(1)} async-done(((bf16[128,2,5632]{2,1,0:T(2,128)(2,1)}), bf16[128,2,5632]{2,1,0:T(2,128)(2,1)S(1)}, u32[]{:S(2)}, u32[]{:S(2)}) %all-to-all-start) | async-done | bytes 2883616 | tf_op jit(solution)/shard_map/all_to_all | solution.py:134
  154.6 3.0 %input_squares.1 = bf16[4,256,512]{2,1,0:T(8,128)(2,1)} custom-call(bf16[128,2,5632]{2,1,0:T(2,128)(2,1)S(1)} %all-to-all-done.arrived_ref, bf16[1536,512]{1,0:T(8,128)(2,1)} %pad_maximum_fusion.1.panel_ref), custom_call_target="tpu_custom_call" | custom-call | tf_op jit(solution)/shard_map/input_squares/pallas_call | solution.py:141
  157.6 4.3 %all-to-all-start.1 = ((bf16[4,256,512]{2,1,0:T(8,128)(2,1)}), bf16[4,256,512]{2,1,0:T(8,128)(2,1)}, u32[]{:S(2)}, u32[]{:S(2)}) async-start(bf16[4,256,512]{2,1,0:T(8,128)(2,1)} %input_squares.1), calls=%async_computation.1 | async-start | bytes 2097152 | tf_op jit(solution)/shard_map/all_to_all | solution.py:155
  161.9 4.5 %output_squares.1 = (bf16[256,256]{1,0:T(8,128)(2,1)S(1)}, bf16[256,256]{1,0:T(8,128)(2,1)S(1)}, bf16[256,256]{1,0:T(8,128)(2,1)S(1)}, bf16[256,256]{1,0:T(8,128)(2,1)S(1)}) custom-call(bf16[128,2,5632]{2,1,0:T(2,128)(2,1)S(1)} %all-to-all-done.arrived_ref, bf16[4096,1024]{1,0:T(8,128)(2,1)} %pad_maximum_fusion.panel_ref), custom_call_target="tpu_custom_call" | custom-call | flops 2147483648 | bytes 8388608 | tf_op jit(solution)/shard_map/output_squares/pallas_call | solution.py:158
  166.4 4.5 %collective-permute-start.6 = (bf16[256,256]{1,0:T(8,128)(2,1)S(1)}, bf16[256,256]{1,0:T(8,128)(2,1)S(1)}, u32[]{:S(2)}, u32[]{:S(2)}) collective-permute-start(bf16[256,256]{1,0:T(8,128)(2,1)S(1)} %get-tuple-element.16), channel_id=1, source_target_pairs={{0,3},{1,0},{2,1},{3,2},{4,7},{5,4},{6,5},{7,6},{8,11},{9,8},{10,9... | collective-permute-start | bytes 393224 | tf_op jit(solution)/shard_map/ppermute | solution.py:23
  170.9 2.5 %collective-permute-start.7 = (bf16[256,256]{1,0:T(8,128)(2,1)S(1)}, bf16[256,256]{1,0:T(8,128)(2,1)S(1)}, u32[]{:S(2)}, u32[]{:S(2)}) collective-permute-start(bf16[256,256]{1,0:T(8,128)(2,1)S(1)} %get-tuple-element.17), channel_id=1, source_target_pairs={{0,2},{1,3},{2,0},{3,1},{4,6},{5,7},{6,4},{7,5},{8,10},{9,11},{10,... | collective-permute-start | bytes 393224 | tf_op jit(solution)/shard_map/ppermute | solution.py:23
  173.4 2.5 %collective-permute-start.8 = (bf16[256,256]{1,0:T(8,128)(2,1)S(1)}, bf16[256,256]{1,0:T(8,128)(2,1)S(1)}, u32[]{:S(2)}, u32[]{:S(2)}) collective-permute-start(bf16[256,256]{1,0:T(8,128)(2,1)S(1)} %get-tuple-element.18), channel_id=1, source_target_pairs={{0,1},{1,2},{2,3},{3,0},{4,5},{5,6},{6,7},{7,4},{8,9},{9,10},{10,1... | collective-permute-start | bytes 393224 | tf_op jit(solution)/shard_map/ppermute | solution.py:23
  175.9 0.0 collective-permute-done.6.refs_1_
  175.9 2.7 %collective-permute-done.7.refs_2_ = bf16[256,256]{1,0:T(8,128)(2,1)S(1)} collective-permute-done((bf16[256,256]{1,0:T(8,128)(2,1)S(1)}, bf16[256,256]{1,0:T(8,128)(2,1)S(1)}, u32[]{:S(2)}, u32[]{:S(2)}) %collective-permute-start.7) | collective-permute-done | bytes 131104 | tf_op jit(solution)/shard_map/ppermute | solution.py:23
  178.6 2.1 %collective-permute-done.8.refs_3_ = bf16[256,256]{1,0:T(8,128)(2,1)S(1)} collective-permute-done((bf16[256,256]{1,0:T(8,128)(2,1)S(1)}, bf16[256,256]{1,0:T(8,128)(2,1)S(1)}, u32[]{:S(2)}, u32[]{:S(2)}) %collective-permute-start.8) | collective-permute-done | bytes 131104 | tf_op jit(solution)/shard_map/ppermute | solution.py:23
  180.6 0.0 all-to-all-done.1.in_ref
  180.6 2.5 %tile.1 = f32[1,512,256]{2,1,0:T(8,128)} custom-call(s32[1]{0:T(128)} %bitcast.me_ref, bf16[4,256,512]{2,1,0:T(8,128)(2,1)} %all-to-all-done.1.in_ref, bf16[256,256]{1,0:T(8,128)(2,1)S(1)} %get-tuple-element.15.refs_0_, bf16[256,256]{1,0:T(8,128)(2,1)S(1)} %collective-permute-done.6.refs_1_, bf16[256,256]{1,0:T(8,128)(2,1)S(1)} %collective-permute-done.7.refs_2_, ...), custom_call_target="tpu_custom_call" | custom-call | tf_op jit(solution)/shard_map/tile/pallas_call | solution.py:179
Async XLA Ops:
  4.2 31.4 %copy-start.1 = (bf16[1,1536,128]{2,1,0:T(8,128)(2,1)S(1)}, bf16[1,1536,128]{2,1,0:T(8,128)(2,1)}, u32[]{:S(2)}) copy-start(bf16[1,1536,128]{2,1,0:T(8,128)(2,1)} %param.8) | copy-start | bytes 1179652
  4.2 150.3 %all-to-all-start = ((bf16[128,2,5632]{2,1,0:T(2,128)(2,1)}), bf16[128,2,5632]{2,1,0:T(2,128)(2,1)S(1)}, u32[]{:S(2)}, u32[]{:S(2)}) async-start(bf16[128,2,5632]{2,1,0:T(2,128)(2,1)} %pack.1), calls=%async_computation | async-start | bytes 5767168 | tf_op jit(solution)/shard_map/all_to_all | solution.py:134
  24.9 115.0 %copy-start = (bf16[1,4096,256]{2,1,0:T(8,128)(2,1)S(1)}, bf16[1,4096,256]{2,1,0:T(8,128)(2,1)}, u32[]{:S(2)}) copy-start(bf16[1,4096,256]{2,1,0:T(8,128)(2,1)} %param.9) | copy-start | bytes 6291460
  25.0 115.0 %collective-permute-start.3 = (bf16[4096,256]{1,0:T(8,128)(2,1)}, bf16[4096,256]{1,0:T(8,128)(2,1)S(1)}, u32[]{:S(2)}, u32[]{:S(2)}) collective-permute-start(bf16[4096,256]{1,0:T(8,128)(2,1)} %bitcast.4), channel_id=1, source_target_pairs={{0,1},{1,2},{2,3},{3,0},{4,5},{5,6},{6,7},{7,4},{8,9},{9,10},{10,1... | collective-permute-start | bytes 6291464 | tf_op jit(solution)/shard_map/ppermute | solution.py:23
  28.2 111.7 %collective-permute-start.4 = (bf16[4096,256]{1,0:T(8,128)(2,1)}, bf16[4096,256]{1,0:T(8,128)(2,1)S(1)}, u32[]{:S(2)}, u32[]{:S(2)}) collective-permute-start(bf16[4096,256]{1,0:T(8,128)(2,1)} %bitcast.5), channel_id=1, source_target_pairs={{0,2},{1,3},{2,0},{3,1},{4,6},{5,7},{6,4},{7,5},{8,10},{9,11},{10,... | collective-permute-start | bytes 6291464 | tf_op jit(solution)/shard_map/ppermute | solution.py:23
  32.6 107.3 %collective-permute-start.5 = (bf16[4096,256]{1,0:T(8,128)(2,1)}, bf16[4096,256]{1,0:T(8,128)(2,1)S(1)}, u32[]{:S(2)}, u32[]{:S(2)}) collective-permute-start(bf16[4096,256]{1,0:T(8,128)(2,1)} %bitcast.6), channel_id=1, source_target_pairs={{0,3},{1,0},{2,1},{3,2},{4,7},{5,4},{6,5},{7,6},{8,11},{9,8},{10,9... | collective-permute-start | bytes 6291464 | tf_op jit(solution)/shard_map/ppermute | solution.py:23
  35.7 92.4 %collective-permute-start = (bf16[1536,128]{1,0:T(8,128)(2,1)S(1)}, bf16[1536,128]{1,0:T(8,128)(2,1)S(1)}, u32[]{:S(2)}, u32[]{:S(2)}) collective-permute-start(bf16[1536,128]{1,0:T(8,128)(2,1)S(1)} %bitcast.8), channel_id=1, source_target_pairs={{0,1},{1,2},{2,3},{3,0},{4,5},{5,6},{6,7},{7,4},{8,9},{9,10},{10,1... | collective-permute-start | bytes 1179656 | tf_op jit(solution)/shard_map/ppermute | solution.py:23
  37.9 99.6 %collective-permute-start.1 = (bf16[1536,128]{1,0:T(8,128)(2,1)S(1)}, bf16[1536,128]{1,0:T(8,128)(2,1)S(1)}, u32[]{:S(2)}, u32[]{:S(2)}) collective-permute-start(bf16[1536,128]{1,0:T(8,128)(2,1)S(1)} %bitcast.9), channel_id=1, source_target_pairs={{0,2},{1,3},{2,0},{3,1},{4,6},{5,7},{6,4},{7,5},{8,10},{9,11},{10,... | collective-permute-start | bytes 1179656 | tf_op jit(solution)/shard_map/ppermute | solution.py:23
  128.1 10.5 %collective-permute-start.2 = (bf16[1536,128]{1,0:T(8,128)(2,1)S(1)}, bf16[1536,128]{1,0:T(8,128)(2,1)S(1)}, u32[]{:S(2)}, u32[]{:S(2)}) collective-permute-start(bf16[1536,128]{1,0:T(8,128)(2,1)S(1)} %bitcast.10), channel_id=1, source_target_pairs={{0,3},{1,0},{2,1},{3,2},{4,7},{5,4},{6,5},{7,6},{8,11},{9,8},{10,9... | collective-permute-start | bytes 1179656 | tf_op jit(solution)/shard_map/ppermute | solution.py:23
  157.6 23.1 %all-to-all-start.1 = ((bf16[4,256,512]{2,1,0:T(8,128)(2,1)}), bf16[4,256,512]{2,1,0:T(8,128)(2,1)}, u32[]{:S(2)}, u32[]{:S(2)}) async-start(bf16[4,256,512]{2,1,0:T(8,128)(2,1)} %input_squares.1), calls=%async_computation.1 | async-start | bytes 2097152 | tf_op jit(solution)/shard_map/all_to_all | solution.py:155
  166.4 9.5 %collective-permute-start.6 = (bf16[256,256]{1,0:T(8,128)(2,1)S(1)}, bf16[256,256]{1,0:T(8,128)(2,1)S(1)}, u32[]{:S(2)}, u32[]{:S(2)}) collective-permute-start(bf16[256,256]{1,0:T(8,128)(2,1)S(1)} %get-tuple-element.16), channel_id=1, source_target_pairs={{0,3},{1,0},{2,1},{3,2},{4,7},{5,4},{6,5},{7,6},{8,11},{9,8},{10,9... | collective-permute-start | bytes 393224 | tf_op jit(solution)/shard_map/ppermute | solution.py:23
  170.9 7.7 %collective-permute-start.7 = (bf16[256,256]{1,0:T(8,128)(2,1)S(1)}, bf16[256,256]{1,0:T(8,128)(2,1)S(1)}, u32[]{:S(2)}, u32[]{:S(2)}) collective-permute-start(bf16[256,256]{1,0:T(8,128)(2,1)S(1)} %get-tuple-element.17), channel_id=1, source_target_pairs={{0,2},{1,3},{2,0},{3,1},{4,6},{5,7},{6,4},{7,5},{8,10},{9,11},{10,... | collective-permute-start | bytes 393224 | tf_op jit(solution)/shard_map/ppermute | solution.py:23
  173.4 7.2 %collective-permute-start.8 = (bf16[256,256]{1,0:T(8,128)(2,1)S(1)}, bf16[256,256]{1,0:T(8,128)(2,1)S(1)}, u32[]{:S(2)}, u32[]{:S(2)}) collective-permute-start(bf16[256,256]{1,0:T(8,128)(2,1)S(1)} %get-tuple-element.18), channel_id=1, source_target_pairs={{0,1},{1,2},{2,3},{3,0},{4,5},{5,6},{6,7},{7,4},{8,9},{9,10},{10,1... | collective-permute-start | bytes 393224 | tf_op jit(solution)/shard_map/ppermute | solution.py:23

commit v3 on v2

--- a/solution.py
+++ b/solution.py
@@ -10,7 +10,6 @@
 
 CHUNK = 512
 VMEM = pl.BlockSpec(memory_space=pltpu.VMEM)
-SMEM = pl.BlockSpec(memory_space=pltpu.SMEM)
 HBM = pl.BlockSpec(memory_space=pltpu.HBM)
 
 
@@ -23,7 +22,7 @@
     return lax.ppermute(values, "help", [(i, (i + steps) % helpers) for i in range(helpers)])
 
 
-def pack_kernel(routing_ref, grad_ref, act_ref, send_ref, rows_ref, packed_ref, in_sems, out_sems):
+def pack_kernel(routing_hbm_ref, grad_ref, act_ref, send_ref, routing_ref, rows_ref, packed_ref, sem, in_sems, out_sems):
     rows, (experts, slots, _) = grad_ref.shape[0], send_ref.shape
     loads, stores, steps, base = [], [], [], 0
     for ref in (grad_ref, act_ref):
@@ -34,8 +33,11 @@
             stores.append(pltpu.make_async_copy(packed_ref.at[:, :, at], send_ref.at[:, :, at], out_sems.at[len(stores)]))
             steps.append((base + k, size))
         base += ref.shape[1]
+    named = pltpu.make_async_copy(routing_hbm_ref, routing_ref, sem)
+    named.start()
     for load in loads:
         load.start()
+    named.wait()
     across = jnp.broadcast_to(routing_ref[...], (rows, rows))
     first, second = (lax.broadcasted_iota(jnp.int32, (rows, rows), axis) for axis in (0, 1))
     earlier = jnp.where((across.T == across) & (first < second), 1.0, 0.0)
@@ -84,10 +86,10 @@
         ref[...] = squares[:, k * ref.shape[1] : (k + 1) * ref.shape[1]]
 
 
-def tile_kernel(helpers, me_ref, in_ref, *refs):
+def tile_kernel(helpers, in_ref, *refs):
     out_refs, (tile_ref, held_ref, sems) = refs[:helpers], refs[helpers:]
     width = tile_ref.shape[1] // helpers
-    me = me_ref[0]
+    me = lax.axis_index("help")
     loads = [
         pltpu.make_async_copy(in_ref.at[lax.rem(me + k, helpers)], held_ref.at[k], sems.at[k]) for k in range(helpers)
     ]
@@ -120,11 +122,13 @@
     send = pl.pallas_call(
         pack_kernel,
         out_shape=jax.ShapeDtypeStruct((experts, slots, width_in + width_out), jnp.bfloat16),
-        in_specs=[VMEM, HBM, HBM],
+        in_specs=[HBM] * 3,
         out_specs=HBM,
         scratch_shapes=[
+            pltpu.VMEM((1, row_count), jnp.int32),
             pltpu.VMEM((row_count, width_in + width_out), jnp.bfloat16),
             pltpu.VMEM((experts, slots, width_in + width_out), jnp.bfloat16),
+            pltpu.SemaphoreType.DMA,
             pltpu.SemaphoreType.DMA((chunks,)),
             pltpu.SemaphoreType.DMA((chunks,)),
         ],
@@ -154,7 +158,6 @@
     )(arrived, pltpu.with_memory_space_constraint(joined_in, pltpu.HBM))
     all_in = lax.all_to_all(own_in, "help", split_axis=0, concat_axis=0, tiled=True)
 
-    me = lax.axis_index("help").astype(jnp.int32)[None]
     own_out = pl.pallas_call(
         output_kernel,
         out_shape=[jax.ShapeDtypeStruct((slots * experts, part_out), jnp.bfloat16)] * helpers,
@@ -179,7 +182,7 @@
     return pl.pallas_call(
         functools.partial(tile_kernel, helpers),
         out_shape=jax.ShapeDtypeStruct((1, panel_in, part_out), jnp.float32),
-        in_specs=[SMEM, HBM] + [VMEM] * helpers,
+        in_specs=[HBM] + [VMEM] * helpers,
         out_specs=VMEM,
         scratch_shapes=[
             pltpu.VMEM((helpers, slots * experts, panel_in), jnp.bfloat16),
@@ -187,7 +190,7 @@
         ],
         compiler_params=params(12),
         name="tile",
-    )(me, pltpu.with_memory_space_constraint(all_in, pltpu.HBM), *all_out)
+    )(pltpu.with_memory_space_constraint(all_in, pltpu.HBM), *all_out)
 
 
 def solution(mesh):

time: 187 us -> 186 us (level)
  no operation moved by 1% of the time
where the time goes in v3:
time: 186 us; the launch traced here: 183 us
  waiting for transfers between devices  110 us (59%)
  starting transfers between devices  53.4 us (29%)
  Pallas kernels  13.8 us (7%)
  other arithmetic  5.27 us (3%)
    ppermute x9, waiting for transfers between devices, shifted(): lax.ppermute(values, 'help', [(i, (i + steps) % helpers) for i in range(h...  99.4 us
    ppermute x9, starting transfers between devices, shifted(): lax.ppermute(values, 'help', [(i, (i + steps) % helpers) for i in range(h...  28.4 us
    all_to_all x1, starting transfers between devices, on_device(): lax.all_to_all(send, 'expert', split_axis=0, concat_axis=0, tiled=True)  20.7 us
    all_to_all x1, waiting for transfers between devices, on_device(): lax.all_to_all(send, 'expert', split_axis=0, concat_axis=0, tiled=True)  10.7 us
    pallas_call x1, Pallas kernels, on_device(): pl.pallas_call(output_kernel, out_shape=[jax.ShapeDtypeStruct((slots * ex...  4.51 us
    all_to_all x1, starting transfers between devices, on_device(): lax.all_to_all(own_in, 'help', split_axis=0, concat_axis=0, tiled=True)  4.27 us
    concatenate x1, other arithmetic, on_device(): jnp.concatenate(out_parts, axis=1)  3.91 us
    pallas_call x1, Pallas kernels, on_device(): pl.pallas_call(pack_kernel, out_shape=jax.ShapeDtypeStruct((experts, slot...  3.79 us
  transfers between devices with their start and end apart: 11, of which 6 were waited for; matrix products, arithmetic and copies ran while one was open for 3% of the time, Pallas kernels for 2%

profile of v3, /device:TPU:1, one launch (start us, length us, event | category | flops | bytes accessed | tf_op | source)
XLA Modules:
  0.0 182.7 jit_solution(2326076339191306298)
XLA Ops:
  0.0 3.8 %pack.1 = bf16[128,2,5632]{2,1,0:T(2,128)(2,1)} custom-call(s32[1,128]{1,0:T(1,128)} %bitcast.11, bf16[128,4096]{1,0:T(8,128)(2,1)} %grad_ref.1, bf16[128,1536]{1,0:T(8,128)(2,1)} %act_ref.1), custom_call_target="tpu_custom_call" | custom-call | tf_op jit(solution)/shard_map/pack/pallas_call | solution.py:122
  3.8 0.0 copy-start.1
  3.8 20.7 %all-to-all-start = ((bf16[128,2,5632]{2,1,0:T(2,128)(2,1)}), bf16[128,2,5632]{2,1,0:T(2,128)(2,1)S(1)}, u32[]{:S(2)}, u32[]{:S(2)}) async-start(bf16[128,2,5632]{2,1,0:T(2,128)(2,1)} %pack.1), calls=%async_computation | async-start | bytes 5767168 | tf_op jit(solution)/shard_map/all_to_all | solution.py:138
  24.5 0.0 copy-start
  24.5 3.3 %collective-permute-start.3 = (bf16[4096,256]{1,0:T(8,128)(2,1)}, bf16[4096,256]{1,0:T(8,128)(2,1)S(1)}, u32[]{:S(2)}, u32[]{:S(2)}) collective-permute-start(bf16[4096,256]{1,0:T(8,128)(2,1)} %bitcast.3), channel_id=1, source_target_pairs={{0,1},{1,2},{2,3},{3,0},{4,5},{5,6},{6,7},{7,4},{8,9},{9,10},{10,1... | collective-permute-start | bytes 6291464 | tf_op jit(solution)/shard_map/ppermute | solution.py:22
  27.8 4.4 %collective-permute-start.4 = (bf16[4096,256]{1,0:T(8,128)(2,1)}, bf16[4096,256]{1,0:T(8,128)(2,1)S(1)}, u32[]{:S(2)}, u32[]{:S(2)}) collective-permute-start(bf16[4096,256]{1,0:T(8,128)(2,1)} %bitcast.4), channel_id=1, source_target_pairs={{0,2},{1,3},{2,0},{3,1},{4,6},{5,7},{6,4},{7,5},{8,10},{9,11},{10,... | collective-permute-start | bytes 6291464 | tf_op jit(solution)/shard_map/ppermute | solution.py:22
  32.2 3.1 %collective-permute-start.5 = (bf16[4096,256]{1,0:T(8,128)(2,1)}, bf16[4096,256]{1,0:T(8,128)(2,1)S(1)}, u32[]{:S(2)}, u32[]{:S(2)}) collective-permute-start(bf16[4096,256]{1,0:T(8,128)(2,1)} %bitcast.5), channel_id=1, source_target_pairs={{0,3},{1,0},{2,1},{3,2},{4,7},{5,4},{6,5},{7,6},{8,11},{9,8},{10,9... | collective-permute-start | bytes 6291464 | tf_op jit(solution)/shard_map/ppermute | solution.py:22
  35.2 0.0 copy-done.1
  35.2 2.2 %collective-permute-start = (bf16[1536,128]{1,0:T(8,128)(2,1)S(1)}, bf16[1536,128]{1,0:T(8,128)(2,1)S(1)}, u32[]{:S(2)}, u32[]{:S(2)}) collective-permute-start(bf16[1536,128]{1,0:T(8,128)(2,1)S(1)} %bitcast.7), channel_id=1, source_target_pairs={{0,1},{1,2},{2,3},{3,0},{4,5},{5,6},{6,7},{7,4},{8,9},{9,10},{10,1... | collective-permute-start | bytes 1179656 | tf_op jit(solution)/shard_map/ppermute | solution.py:22
  37.5 2.8 %collective-permute-start.1 = (bf16[1536,128]{1,0:T(8,128)(2,1)S(1)}, bf16[1536,128]{1,0:T(8,128)(2,1)S(1)}, u32[]{:S(2)}, u32[]{:S(2)}) collective-permute-start(bf16[1536,128]{1,0:T(8,128)(2,1)S(1)} %bitcast.8), channel_id=1, source_target_pairs={{0,2},{1,3},{2,0},{3,1},{4,6},{5,7},{6,4},{7,5},{8,10},{9,11},{10,... | collective-permute-start | bytes 1179656 | tf_op jit(solution)/shard_map/ppermute | solution.py:22
  40.3 87.4 %collective-permute-done = bf16[1536,128]{1,0:T(8,128)(2,1)S(1)} collective-permute-done((bf16[1536,128]{1,0:T(8,128)(2,1)S(1)}, bf16[1536,128]{1,0:T(8,128)(2,1)S(1)}, u32[]{:S(2)}, u32[]{:S(2)}) %collective-permute-start) | collective-permute-done | bytes 393248 | tf_op jit(solution)/shard_map/ppermute | solution.py:22
  127.6 3.2 %collective-permute-start.2 = (bf16[1536,128]{1,0:T(8,128)(2,1)S(1)}, bf16[1536,128]{1,0:T(8,128)(2,1)S(1)}, u32[]{:S(2)}, u32[]{:S(2)}) collective-permute-start(bf16[1536,128]{1,0:T(8,128)(2,1)S(1)} %bitcast.9), channel_id=1, source_target_pairs={{0,3},{1,0},{2,1},{3,2},{4,7},{5,4},{6,5},{7,6},{8,11},{9,8},{10,9... | collective-permute-start | bytes 1179656 | tf_op jit(solution)/shard_map/ppermute | solution.py:22
  130.9 6.2 %collective-permute-done.1 = bf16[1536,128]{1,0:T(8,128)(2,1)S(1)} collective-permute-done((bf16[1536,128]{1,0:T(8,128)(2,1)S(1)}, bf16[1536,128]{1,0:T(8,128)(2,1)S(1)}, u32[]{:S(2)}, u32[]{:S(2)}) %collective-permute-start.1) | collective-permute-done | bytes 393248 | tf_op jit(solution)/shard_map/ppermute | solution.py:22
  137.1 1.0 collective-permute-done.2
  138.1 1.4 pad_maximum_fusion.1.panel_ref
  139.5 0.0 collective-permute-done.3
  139.5 0.0 collective-permute-done.4
  139.5 0.0 collective-permute-done.5
  139.5 0.0 copy-done
  139.5 3.9 %pad_maximum_fusion.panel_ref = bf16[4096,1024]{1,0:T(8,128)(2,1)} fusion(bf16[4096,256]{1,0:T(8,128)(2,1)S(1)} %collective-permute-done.5, bf16[4096,256]{1,0:T(8,128)(2,1)S(1)} %collective-permute-done.4, bf16[4096,256]{1,0:T(8,128)(2,1)S(1)} %collective-permute-done.3, bf16[4096,256]{1,0:T(8,128)(2,1)S(1)} %bitcast.6), kind=kLoop, calls=%fused_computation | loop fusion | flops 33554432 | bytes 16777216 | tf_op jit(solution)/shard_map/concatenate | solution.py:142
  143.4 10.7 %all-to-all-done.arrived_ref = bf16[128,2,5632]{2,1,0:T(2,128)(2,1)S(1)} async-done(((bf16[128,2,5632]{2,1,0:T(2,128)(2,1)}), bf16[128,2,5632]{2,1,0:T(2,128)(2,1)S(1)}, u32[]{:S(2)}, u32[]{:S(2)}) %all-to-all-start) | async-done | bytes 2883616 | tf_op jit(solution)/shard_map/all_to_all | solution.py:138
  154.2 3.0 %input_squares.1 = bf16[4,256,512]{2,1,0:T(8,128)(2,1)} custom-call(bf16[128,2,5632]{2,1,0:T(2,128)(2,1)S(1)} %all-to-all-done.arrived_ref, bf16[1536,512]{1,0:T(8,128)(2,1)} %pad_maximum_fusion.1.panel_ref), custom_call_target="tpu_custom_call" | custom-call | tf_op jit(solution)/shard_map/input_squares/pallas_call | solution.py:145
  157.2 4.3 %all-to-all-start.1 = ((bf16[4,256,512]{2,1,0:T(8,128)(2,1)}), bf16[4,256,512]{2,1,0:T(8,128)(2,1)}, u32[]{:S(2)}, u32[]{:S(2)}) async-start(bf16[4,256,512]{2,1,0:T(8,128)(2,1)} %input_squares.1), calls=%async_computation.1 | async-start | bytes 2097152 | tf_op jit(solution)/shard_map/all_to_all | solution.py:159
  161.4 4.5 %output_squares.1 = (bf16[256,256]{1,0:T(8,128)(2,1)S(1)}, bf16[256,256]{1,0:T(8,128)(2,1)S(1)}, bf16[256,256]{1,0:T(8,128)(2,1)S(1)}, bf16[256,256]{1,0:T(8,128)(2,1)S(1)}) custom-call(bf16[128,2,5632]{2,1,0:T(2,128)(2,1)S(1)} %all-to-all-done.arrived_ref, bf16[4096,1024]{1,0:T(8,128)(2,1)} %pad_maximum_fusion.panel_ref), custom_call_target="tpu_custom_call" | custom-call | flops 2147483648 | bytes 8388608 | tf_op jit(solution)/shard_map/output_squares/pallas_call | solution.py:161
  166.0 4.5 %collective-permute-start.6 = (bf16[256,256]{1,0:T(8,128)(2,1)S(1)}, bf16[256,256]{1,0:T(8,128)(2,1)S(1)}, u32[]{:S(2)}, u32[]{:S(2)}) collective-permute-start(bf16[256,256]{1,0:T(8,128)(2,1)S(1)} %get-tuple-element.16), channel_id=1, source_target_pairs={{0,3},{1,0},{2,1},{3,2},{4,7},{5,4},{6,5},{7,6},{8,11},{9,8},{10,9... | collective-permute-start | bytes 393224 | tf_op jit(solution)/shard_map/ppermute | solution.py:22
  170.5 2.5 %collective-permute-start.7 = (bf16[256,256]{1,0:T(8,128)(2,1)S(1)}, bf16[256,256]{1,0:T(8,128)(2,1)S(1)}, u32[]{:S(2)}, u32[]{:S(2)}) collective-permute-start(bf16[256,256]{1,0:T(8,128)(2,1)S(1)} %get-tuple-element.17), channel_id=1, source_target_pairs={{0,2},{1,3},{2,0},{3,1},{4,6},{5,7},{6,4},{7,5},{8,10},{9,11},{10,... | collective-permute-start | bytes 393224 | tf_op jit(solution)/shard_map/ppermute | solution.py:22
  173.0 2.5 %collective-permute-start.8 = (bf16[256,256]{1,0:T(8,128)(2,1)S(1)}, bf16[256,256]{1,0:T(8,128)(2,1)S(1)}, u32[]{:S(2)}, u32[]{:S(2)}) collective-permute-start(bf16[256,256]{1,0:T(8,128)(2,1)S(1)} %get-tuple-element.18), channel_id=1, source_target_pairs={{0,1},{1,2},{2,3},{3,0},{4,5},{5,6},{6,7},{7,4},{8,9},{9,10},{10,1... | collective-permute-start | bytes 393224 | tf_op jit(solution)/shard_map/ppermute | solution.py:22
  175.5 0.0 collective-permute-done.6.refs_1_
  175.5 2.7 %collective-permute-done.7.refs_2_ = bf16[256,256]{1,0:T(8,128)(2,1)S(1)} collective-permute-done((bf16[256,256]{1,0:T(8,128)(2,1)S(1)}, bf16[256,256]{1,0:T(8,128)(2,1)S(1)}, u32[]{:S(2)}, u32[]{:S(2)}) %collective-permute-start.7) | collective-permute-done | bytes 131104 | tf_op jit(solution)/shard_map/ppermute | solution.py:22
  178.2 2.1 %collective-permute-done.8.refs_3_ = bf16[256,256]{1,0:T(8,128)(2,1)S(1)} collective-permute-done((bf16[256,256]{1,0:T(8,128)(2,1)S(1)}, bf16[256,256]{1,0:T(8,128)(2,1)S(1)}, u32[]{:S(2)}, u32[]{:S(2)}) %collective-permute-start.8) | collective-permute-done | bytes 131104 | tf_op jit(solution)/shard_map/ppermute | solution.py:22
  180.2 0.0 all-to-all-done.1.in_ref
  180.2 2.5 %tile.1 = f32[1,512,256]{2,1,0:T(8,128)} custom-call(bf16[4,256,512]{2,1,0:T(8,128)(2,1)} %all-to-all-done.1.in_ref, bf16[256,256]{1,0:T(8,128)(2,1)S(1)} %get-tuple-element.15.refs_0_, bf16[256,256]{1,0:T(8,128)(2,1)S(1)} %collective-permute-done.6.refs_1_, bf16[256,256]{1,0:T(8,128)(2,1)S(1)} %collective-permute-done.7.refs_2_, ...), custom_call_target="tpu_custom_call" | custom-call | tf_op jit(solution)/shard_map/tile/pallas_call | solution.py:182
Async XLA Ops:
  3.8 31.4 %copy-start.1 = (bf16[1,1536,128]{2,1,0:T(8,128)(2,1)S(1)}, bf16[1,1536,128]{2,1,0:T(8,128)(2,1)}, u32[]{:S(2)}) copy-start(bf16[1,1536,128]{2,1,0:T(8,128)(2,1)} %param.8) | copy-start | bytes 1179652
  3.8 150.3 %all-to-all-start = ((bf16[128,2,5632]{2,1,0:T(2,128)(2,1)}), bf16[128,2,5632]{2,1,0:T(2,128)(2,1)S(1)}, u32[]{:S(2)}, u32[]{:S(2)}) async-start(bf16[128,2,5632]{2,1,0:T(2,128)(2,1)} %pack.1), calls=%async_computation | async-start | bytes 5767168 | tf_op jit(solution)/shard_map/all_to_all | solution.py:138
  24.5 115.0 %copy-start = (bf16[1,4096,256]{2,1,0:T(8,128)(2,1)S(1)}, bf16[1,4096,256]{2,1,0:T(8,128)(2,1)}, u32[]{:S(2)}) copy-start(bf16[1,4096,256]{2,1,0:T(8,128)(2,1)} %param.9) | copy-start | bytes 6291460
  24.5 115.0 %collective-permute-start.3 = (bf16[4096,256]{1,0:T(8,128)(2,1)}, bf16[4096,256]{1,0:T(8,128)(2,1)S(1)}, u32[]{:S(2)}, u32[]{:S(2)}) collective-permute-start(bf16[4096,256]{1,0:T(8,128)(2,1)} %bitcast.3), channel_id=1, source_target_pairs={{0,1},{1,2},{2,3},{3,0},{4,5},{5,6},{6,7},{7,4},{8,9},{9,10},{10,1... | collective-permute-start | bytes 6291464 | tf_op jit(solution)/shard_map/ppermute | solution.py:22
  27.8 111.7 %collective-permute-start.4 = (bf16[4096,256]{1,0:T(8,128)(2,1)}, bf16[4096,256]{1,0:T(8,128)(2,1)S(1)}, u32[]{:S(2)}, u32[]{:S(2)}) collective-permute-start(bf16[4096,256]{1,0:T(8,128)(2,1)} %bitcast.4), channel_id=1, source_target_pairs={{0,2},{1,3},{2,0},{3,1},{4,6},{5,7},{6,4},{7,5},{8,10},{9,11},{10,... | collective-permute-start | bytes 6291464 | tf_op jit(solution)/shard_map/ppermute | solution.py:22
  32.2 107.3 %collective-permute-start.5 = (bf16[4096,256]{1,0:T(8,128)(2,1)}, bf16[4096,256]{1,0:T(8,128)(2,1)S(1)}, u32[]{:S(2)}, u32[]{:S(2)}) collective-permute-start(bf16[4096,256]{1,0:T(8,128)(2,1)} %bitcast.5), channel_id=1, source_target_pairs={{0,3},{1,0},{2,1},{3,2},{4,7},{5,4},{6,5},{7,6},{8,11},{9,8},{10,9... | collective-permute-start | bytes 6291464 | tf_op jit(solution)/shard_map/ppermute | solution.py:22
  35.2 92.4 %collective-permute-start = (bf16[1536,128]{1,0:T(8,128)(2,1)S(1)}, bf16[1536,128]{1,0:T(8,128)(2,1)S(1)}, u32[]{:S(2)}, u32[]{:S(2)}) collective-permute-start(bf16[1536,128]{1,0:T(8,128)(2,1)S(1)} %bitcast.7), channel_id=1, source_target_pairs={{0,1},{1,2},{2,3},{3,0},{4,5},{5,6},{6,7},{7,4},{8,9},{9,10},{10,1... | collective-permute-start | bytes 1179656 | tf_op jit(solution)/shard_map/ppermute | solution.py:22
  37.5 99.6 %collective-permute-start.1 = (bf16[1536,128]{1,0:T(8,128)(2,1)S(1)}, bf16[1536,128]{1,0:T(8,128)(2,1)S(1)}, u32[]{:S(2)}, u32[]{:S(2)}) collective-permute-start(bf16[1536,128]{1,0:T(8,128)(2,1)S(1)} %bitcast.8), channel_id=1, source_target_pairs={{0,2},{1,3},{2,0},{3,1},{4,6},{5,7},{6,4},{7,5},{8,10},{9,11},{10,... | collective-permute-start | bytes 1179656 | tf_op jit(solution)/shard_map/ppermute | solution.py:22
  127.6 10.5 %collective-permute-start.2 = (bf16[1536,128]{1,0:T(8,128)(2,1)S(1)}, bf16[1536,128]{1,0:T(8,128)(2,1)S(1)}, u32[]{:S(2)}, u32[]{:S(2)}) collective-permute-start(bf16[1536,128]{1,0:T(8,128)(2,1)S(1)} %bitcast.9), channel_id=1, source_target_pairs={{0,3},{1,0},{2,1},{3,2},{4,7},{5,4},{6,5},{7,6},{8,11},{9,8},{10,9... | collective-permute-start | bytes 1179656 | tf_op jit(solution)/shard_map/ppermute | solution.py:22
  157.2 23.1 %all-to-all-start.1 = ((bf16[4,256,512]{2,1,0:T(8,128)(2,1)}), bf16[4,256,512]{2,1,0:T(8,128)(2,1)}, u32[]{:S(2)}, u32[]{:S(2)}) async-start(bf16[4,256,512]{2,1,0:T(8,128)(2,1)} %input_squares.1), calls=%async_computation.1 | async-start | bytes 2097152 | tf_op jit(solution)/shard_map/all_to_all | solution.py:159
  166.0 9.5 %collective-permute-start.6 = (bf16[256,256]{1,0:T(8,128)(2,1)S(1)}, bf16[256,256]{1,0:T(8,128)(2,1)S(1)}, u32[]{:S(2)}, u32[]{:S(2)}) collective-permute-start(bf16[256,256]{1,0:T(8,128)(2,1)S(1)} %get-tuple-element.16), channel_id=1, source_target_pairs={{0,3},{1,0},{2,1},{3,2},{4,7},{5,4},{6,5},{7,6},{8,11},{9,8},{10,9... | collective-permute-start | bytes 393224 | tf_op jit(solution)/shard_map/ppermute | solution.py:22
  170.5 7.7 %collective-permute-start.7 = (bf16[256,256]{1,0:T(8,128)(2,1)S(1)}, bf16[256,256]{1,0:T(8,128)(2,1)S(1)}, u32[]{:S(2)}, u32[]{:S(2)}) collective-permute-start(bf16[256,256]{1,0:T(8,128)(2,1)S(1)} %get-tuple-element.17), channel_id=1, source_target_pairs={{0,2},{1,3},{2,0},{3,1},{4,6},{5,7},{6,4},{7,5},{8,10},{9,11},{10,... | collective-permute-start | bytes 393224 | tf_op jit(solution)/shard_map/ppermute | solution.py:22
  173.0 7.2 %collective-permute-start.8 = (bf16[256,256]{1,0:T(8,128)(2,1)S(1)}, bf16[256,256]{1,0:T(8,128)(2,1)S(1)}, u32[]{:S(2)}, u32[]{:S(2)}) collective-permute-start(bf16[256,256]{1,0:T(8,128)(2,1)S(1)} %get-tuple-element.18), channel_id=1, source_target_pairs={{0,1},{1,2},{2,3},{3,0},{4,5},{5,6},{6,7},{7,4},{8,9},{9,10},{10,1... | collective-permute-start | bytes 393224 | tf_op jit(solution)/shard_map/ppermute | solution.py:22

commit v4 on v1

--- a/solution.py
+++ b/solution.py
@@ -10,7 +10,6 @@
 
 CHUNK = 512
 VMEM = pl.BlockSpec(memory_space=pltpu.VMEM)
-SMEM = pl.BlockSpec(memory_space=pltpu.SMEM)
 HBM = pl.BlockSpec(memory_space=pltpu.HBM)
 
 
@@ -23,7 +22,7 @@
     return lax.ppermute(values, "help", [(i, (i + steps) % helpers) for i in range(helpers)])
 
 
-def pack_kernel(routing_ref, grad_ref, act_ref, send_ref, rows_ref, packed_ref, in_sems, out_sems):
+def pack_kernel(routing_hbm_ref, grad_ref, act_ref, send_ref, routing_ref, rows_ref, packed_ref, sem, in_sems, out_sems):
     rows, (experts, slots, _) = grad_ref.shape[0], send_ref.shape
     loads, stores, steps, base = [], [], [], 0
     for ref in (grad_ref, act_ref):
@@ -34,8 +33,11 @@
             stores.append(pltpu.make_async_copy(packed_ref.at[:, :, at], send_ref.at[:, :, at], out_sems.at[len(stores)]))
             steps.append((base + k, size))
         base += ref.shape[1]
+    named = pltpu.make_async_copy(routing_hbm_ref, routing_ref, sem)
+    named.start()
     for load in loads:
         load.start()
+    named.wait()
     across = jnp.broadcast_to(routing_ref[...], (rows, rows))
     first, second = (lax.broadcasted_iota(jnp.int32, (rows, rows), axis) for axis in (0, 1))
     earlier = jnp.where((across.T == across) & (first < second), 1.0, 0.0)
@@ -84,10 +86,18 @@
         ref[...] = squares[:, k * ref.shape[1] : (k + 1) * ref.shape[1]]
 
 
-def tile_kernel(helpers, me_ref, in_ref, *refs):
+def early_kernel(in_ref, held_ref, sems):
+    copies = [pltpu.make_async_copy(in_ref.at[k], held_ref.at[k], sems.at[k]) for k in range(in_ref.shape[0])]
+    for copy in copies:
+        copy.start()
+    for copy in copies:
+        copy.wait()
+
+
+def tile_kernel(helpers, in_ref, *refs):
     out_refs, tile_ref = refs[:-1], refs[-1]
     width = tile_ref.shape[1] // helpers
-    me = me_ref[0]
+    me = lax.axis_index("help")
     for j in range(helpers):
         total = None
         for k in range(helpers):
@@ -113,11 +123,13 @@
     send = pl.pallas_call(
         pack_kernel,
         out_shape=jax.ShapeDtypeStruct((experts, slots, width_in + width_out), jnp.bfloat16),
-        in_specs=[VMEM, HBM, HBM],
+        in_specs=[HBM] * 3,
         out_specs=HBM,
         scratch_shapes=[
+            pltpu.VMEM((1, row_count), jnp.int32),
             pltpu.VMEM((row_count, width_in + width_out), jnp.bfloat16),
             pltpu.VMEM((experts, slots, width_in + width_out), jnp.bfloat16),
+            pltpu.SemaphoreType.DMA,
             pltpu.SemaphoreType.DMA((chunks,)),
             pltpu.SemaphoreType.DMA((chunks,)),
         ],
@@ -147,7 +159,6 @@
     )(arrived, pltpu.with_memory_space_constraint(joined_in, pltpu.HBM))
     all_in = lax.all_to_all(own_in, "help", split_axis=0, concat_axis=0, tiled=True)
 
-    me = lax.axis_index("help").astype(jnp.int32)[None]
     own_out = pl.pallas_call(
         output_kernel,
         out_shape=[jax.ShapeDtypeStruct((slots * experts, part_out), jnp.bfloat16)] * helpers,
@@ -165,16 +176,27 @@
         ),
         name="output_squares",
     )(arrived, pltpu.with_memory_space_constraint(joined_out, pltpu.HBM))
-    all_out = [own_out[0]] + [shifted(own_out[k], helpers - k) for k in range(1, helpers)]
-
+    all_out = [own_out[0]]
+    for k in range(1, helpers):
+        all_out.append(shifted(own_out[k], helpers - k))
+
+    all_in = pl.pallas_call(
+        early_kernel,
+        out_shape=jax.ShapeDtypeStruct(all_in.shape, all_in.dtype),
+        in_specs=[HBM],
+        out_specs=VMEM,
+        scratch_shapes=[pltpu.SemaphoreType.DMA((helpers,))],
+        compiler_params=params(8),
+        name="early",
+    )(pltpu.with_memory_space_constraint(all_in, pltpu.HBM))
     return pl.pallas_call(
         functools.partial(tile_kernel, helpers),
         out_shape=jax.ShapeDtypeStruct((1, panel_in, part_out), jnp.float32),
-        in_specs=[SMEM] + [VMEM] * (helpers + 1),
+        in_specs=[VMEM] * (helpers + 1),
         out_specs=VMEM,
         compiler_params=params(12),
         name="tile",
-    )(me, all_in, *all_out)
+    )(all_in, *all_out)
 
 
 def solution(mesh):

time: 187 us -> 185 us (0.989)
  transfers between devices with their start and end apart: 11 -> 11, of which waited for: 6 -> 6; matrix products, arithmetic and copies ran while one was open for 3% -> 3% of each run, Pallas kernels for 2% -> 3%
where the time goes in v4:
time: 185 us; the launch traced here: 182 us
  waiting for transfers between devices  109 us (59%)
  starting transfers between devices  53.4 us (29%)
  Pallas kernels  13.8 us (7%)
  other arithmetic  5.27 us (3%)
    ppermute x9, waiting for transfers between devices, shifted(): lax.ppermute(values, 'help', [(i, (i + steps) % helpers) for i in range(h...  98.1 us
    ppermute x9, starting transfers between devices, shifted(): lax.ppermute(values, 'help', [(i, (i + steps) % helpers) for i in range(h...  28.4 us
    all_to_all x1, starting transfers between devices, on_device(): lax.all_to_all(send, 'expert', split_axis=0, concat_axis=0, tiled=True)  20.7 us
    all_to_all x1, waiting for transfers between devices, on_device(): lax.all_to_all(send, 'expert', split_axis=0, concat_axis=0, tiled=True)  10.7 us
    pallas_call x1, Pallas kernels, on_device(): pl.pallas_call(output_kernel, out_shape=[jax.ShapeDtypeStruct((slots * ex...  4.51 us
    all_to_all x1, starting transfers between devices, on_device(): lax.all_to_all(own_in, 'help', split_axis=0, concat_axis=0, tiled=True)  4.27 us
    concatenate x1, other arithmetic, on_device(): jnp.concatenate(out_parts, axis=1)  3.91 us
    pallas_call x1, Pallas kernels, on_device(): pl.pallas_call(pack_kernel, out_shape=jax.ShapeDtypeStruct((experts, slot...  3.79 us
  transfers between devices with their start and end apart: 11, of which 6 were waited for; matrix products, arithmetic and copies ran while one was open for 3% of the time, Pallas kernels for 3%

profile of v4, /device:TPU:1, one launch (start us, length us, event | category | flops | bytes accessed | tf_op | source)
XLA Modules:
  0.0 181.5 jit_solution(15603940819595266012)
XLA Ops:
  0.0 3.8 %pack.1 = bf16[128,2,5632]{2,1,0:T(2,128)(2,1)} custom-call(s32[1,128]{1,0:T(1,128)} %bitcast.11, bf16[128,4096]{1,0:T(8,128)(2,1)} %grad_ref.1, bf16[128,1536]{1,0:T(8,128)(2,1)} %act_ref.1), custom_call_target="tpu_custom_call" | custom-call | tf_op jit(solution)/shard_map/pack/pallas_call | solution.py:123
  3.8 0.0 copy-start.1
  3.8 20.7 %all-to-all-start = ((bf16[128,2,5632]{2,1,0:T(2,128)(2,1)}), bf16[128,2,5632]{2,1,0:T(2,128)(2,1)S(1)}, u32[]{:S(2)}, u32[]{:S(2)}) async-start(bf16[128,2,5632]{2,1,0:T(2,128)(2,1)} %pack.1), calls=%async_computation | async-start | bytes 5767168 | tf_op jit(solution)/shard_map/all_to_all | solution.py:139
  24.5 0.0 copy-start
  24.5 3.3 %collective-permute-start.3 = (bf16[4096,256]{1,0:T(8,128)(2,1)}, bf16[4096,256]{1,0:T(8,128)(2,1)S(1)}, u32[]{:S(2)}, u32[]{:S(2)}) collective-permute-start(bf16[4096,256]{1,0:T(8,128)(2,1)} %bitcast.3), channel_id=1, source_target_pairs={{0,1},{1,2},{2,3},{3,0},{4,5},{5,6},{6,7},{7,4},{8,9},{9,10},{10,1... | collective-permute-start | bytes 6291464 | tf_op jit(solution)/shard_map/ppermute | solution.py:22
  27.8 4.4 %collective-permute-start.4 = (bf16[4096,256]{1,0:T(8,128)(2,1)}, bf16[4096,256]{1,0:T(8,128)(2,1)S(1)}, u32[]{:S(2)}, u32[]{:S(2)}) collective-permute-start(bf16[4096,256]{1,0:T(8,128)(2,1)} %bitcast.4), channel_id=1, source_target_pairs={{0,2},{1,3},{2,0},{3,1},{4,6},{5,7},{6,4},{7,5},{8,10},{9,11},{10,... | collective-permute-start | bytes 6291464 | tf_op jit(solution)/shard_map/ppermute | solution.py:22
  32.2 3.1 %collective-permute-start.5 = (bf16[4096,256]{1,0:T(8,128)(2,1)}, bf16[4096,256]{1,0:T(8,128)(2,1)S(1)}, u32[]{:S(2)}, u32[]{:S(2)}) collective-permute-start(bf16[4096,256]{1,0:T(8,128)(2,1)} %bitcast.5), channel_id=1, source_target_pairs={{0,3},{1,0},{2,1},{3,2},{4,7},{5,4},{6,5},{7,6},{8,11},{9,8},{10,9... | collective-permute-start | bytes 6291464 | tf_op jit(solution)/shard_map/ppermute | solution.py:22
  35.2 0.0 copy-done.1
  35.2 2.2 %collective-permute-start = (bf16[1536,128]{1,0:T(8,128)(2,1)S(1)}, bf16[1536,128]{1,0:T(8,128)(2,1)S(1)}, u32[]{:S(2)}, u32[]{:S(2)}) collective-permute-start(bf16[1536,128]{1,0:T(8,128)(2,1)S(1)} %bitcast.7), channel_id=1, source_target_pairs={{0,1},{1,2},{2,3},{3,0},{4,5},{5,6},{6,7},{7,4},{8,9},{9,10},{10,1... | collective-permute-start | bytes 1179656 | tf_op jit(solution)/shard_map/ppermute | solution.py:22
  37.5 2.8 %collective-permute-start.1 = (bf16[1536,128]{1,0:T(8,128)(2,1)S(1)}, bf16[1536,128]{1,0:T(8,128)(2,1)S(1)}, u32[]{:S(2)}, u32[]{:S(2)}) collective-permute-start(bf16[1536,128]{1,0:T(8,128)(2,1)S(1)} %bitcast.8), channel_id=1, source_target_pairs={{0,2},{1,3},{2,0},{3,1},{4,6},{5,7},{6,4},{7,5},{8,10},{9,11},{10,... | collective-permute-start | bytes 1179656 | tf_op jit(solution)/shard_map/ppermute | solution.py:22
  40.3 87.4 %collective-permute-done = bf16[1536,128]{1,0:T(8,128)(2,1)S(1)} collective-permute-done((bf16[1536,128]{1,0:T(8,128)(2,1)S(1)}, bf16[1536,128]{1,0:T(8,128)(2,1)S(1)}, u32[]{:S(2)}, u32[]{:S(2)}) %collective-permute-start) | collective-permute-done | bytes 393248 | tf_op jit(solution)/shard_map/ppermute | solution.py:22
  127.6 3.2 %collective-permute-start.2 = (bf16[1536,128]{1,0:T(8,128)(2,1)S(1)}, bf16[1536,128]{1,0:T(8,128)(2,1)S(1)}, u32[]{:S(2)}, u32[]{:S(2)}) collective-permute-start(bf16[1536,128]{1,0:T(8,128)(2,1)S(1)} %bitcast.9), channel_id=1, source_target_pairs={{0,3},{1,0},{2,1},{3,2},{4,7},{5,4},{6,5},{7,6},{8,11},{9,8},{10,9... | collective-permute-start | bytes 1179656 | tf_op jit(solution)/shard_map/ppermute | solution.py:22
  130.9 6.2 %collective-permute-done.1 = bf16[1536,128]{1,0:T(8,128)(2,1)S(1)} collective-permute-done((bf16[1536,128]{1,0:T(8,128)(2,1)S(1)}, bf16[1536,128]{1,0:T(8,128)(2,1)S(1)}, u32[]{:S(2)}, u32[]{:S(2)}) %collective-permute-start.1) | collective-permute-done | bytes 393248 | tf_op jit(solution)/shard_map/ppermute | solution.py:22
  137.1 1.0 collective-permute-done.2
  138.1 1.4 pad_maximum_fusion.1.panel_ref
  139.5 0.0 collective-permute-done.3
  139.5 0.0 collective-permute-done.4
  139.5 0.0 collective-permute-done.5
  139.5 3.9 %pad_maximum_fusion.panel_ref = bf16[4096,1024]{1,0:T(8,128)(2,1)} fusion(bf16[4096,256]{1,0:T(8,128)(2,1)S(1)} %collective-permute-done.5, bf16[4096,256]{1,0:T(8,128)(2,1)S(1)} %collective-permute-done.4, bf16[4096,256]{1,0:T(8,128)(2,1)S(1)} %collective-permute-done.3, bf16[4096,256]{1,0:T(8,128)(2,1)S(1)} %bitcast.6), kind=kLoop, calls=%fused_computation | loop fusion | flops 33554432 | bytes 16777216 | tf_op jit(solution)/shard_map/concatenate | solution.py:143
  143.4 10.7 %all-to-all-done.arrived_ref = bf16[128,2,5632]{2,1,0:T(2,128)(2,1)S(1)} async-done(((bf16[128,2,5632]{2,1,0:T(2,128)(2,1)}), bf16[128,2,5632]{2,1,0:T(2,128)(2,1)S(1)}, u32[]{:S(2)}, u32[]{:S(2)}) %all-to-all-start) | async-done | bytes 2883616 | tf_op jit(solution)/shard_map/all_to_all | solution.py:139
  154.2 3.0 %input_squares.1 = bf16[4,256,512]{2,1,0:T(8,128)(2,1)} custom-call(bf16[128,2,5632]{2,1,0:T(2,128)(2,1)S(1)} %all-to-all-done.arrived_ref, bf16[1536,512]{1,0:T(8,128)(2,1)} %pad_maximum_fusion.1.panel_ref), custom_call_target="tpu_custom_call" | custom-call | tf_op jit(solution)/shard_map/input_squares/pallas_call | solution.py:146
  157.2 4.3 %all-to-all-start.1 = ((bf16[4,256,512]{2,1,0:T(8,128)(2,1)}), bf16[4,256,512]{2,1,0:T(8,128)(2,1)}, u32[]{:S(2)}, u32[]{:S(2)}) async-start(bf16[4,256,512]{2,1,0:T(8,128)(2,1)} %input_squares.1), calls=%async_computation.1 | async-start | bytes 2097152 | tf_op jit(solution)/shard_map/all_to_all | solution.py:160
  161.4 4.5 %output_squares.1 = (bf16[256,256]{1,0:T(8,128)(2,1)S(1)}, bf16[256,256]{1,0:T(8,128)(2,1)S(1)}, bf16[256,256]{1,0:T(8,128)(2,1)S(1)}, bf16[256,256]{1,0:T(8,128)(2,1)S(1)}) custom-call(bf16[128,2,5632]{2,1,0:T(2,128)(2,1)S(1)} %all-to-all-done.arrived_ref, bf16[4096,1024]{1,0:T(8,128)(2,1)} %pad_maximum_fusion.panel_ref), custom_call_target="tpu_custom_call" | custom-call | flops 2147483648 | bytes 8388608 | tf_op jit(solution)/shard_map/output_squares/pallas_call | solution.py:162
  166.0 4.5 %collective-permute-start.6 = (bf16[256,256]{1,0:T(8,128)(2,1)S(1)}, bf16[256,256]{1,0:T(8,128)(2,1)S(1)}, u32[]{:S(2)}, u32[]{:S(2)}) collective-permute-start(bf16[256,256]{1,0:T(8,128)(2,1)S(1)} %get-tuple-element.16), channel_id=1, source_target_pairs={{0,3},{1,0},{2,1},{3,2},{4,7},{5,4},{6,5},{7,6},{8,11},{9,8},{10,9... | collective-permute-start | bytes 393224 | tf_op jit(solution)/shard_map/ppermute | solution.py:22
  170.5 2.5 %collective-permute-start.7 = (bf16[256,256]{1,0:T(8,128)(2,1)S(1)}, bf16[256,256]{1,0:T(8,128)(2,1)S(1)}, u32[]{:S(2)}, u32[]{:S(2)}) collective-permute-start(bf16[256,256]{1,0:T(8,128)(2,1)S(1)} %get-tuple-element.17), channel_id=1, source_target_pairs={{0,2},{1,3},{2,0},{3,1},{4,6},{5,7},{6,4},{7,5},{8,10},{9,11},{10,... | collective-permute-start | bytes 393224 | tf_op jit(solution)/shard_map/ppermute | solution.py:22
  173.0 2.5 %collective-permute-start.8 = (bf16[256,256]{1,0:T(8,128)(2,1)S(1)}, bf16[256,256]{1,0:T(8,128)(2,1)S(1)}, u32[]{:S(2)}, u32[]{:S(2)}) collective-permute-start(bf16[256,256]{1,0:T(8,128)(2,1)S(1)} %get-tuple-element.18), channel_id=1, source_target_pairs={{0,1},{1,2},{2,3},{3,0},{4,5},{5,6},{6,7},{7,4},{8,9},{9,10},{10,1... | collective-permute-start | bytes 393224 | tf_op jit(solution)/shard_map/ppermute | solution.py:22
  175.5 0.0 all-to-all-done.1.in_ref
  175.5 1.2 early.1.in_ref
  176.7 0.0 collective-permute-done.6.refs_1_
  176.7 1.4 collective-permute-done.7.refs_2_
  178.2 2.1 %collective-permute-done.8.refs_3_ = bf16[256,256]{1,0:T(8,128)(2,1)S(1)} collective-permute-done((bf16[256,256]{1,0:T(8,128)(2,1)S(1)}, bf16[256,256]{1,0:T(8,128)(2,1)S(1)}, u32[]{:S(2)}, u32[]{:S(2)}) %collective-permute-start.8) | collective-permute-done | bytes 131104 | tf_op jit(solution)/shard_map/ppermute | solution.py:22
  180.2 1.3 tile.1
  (1 shorter events, 0.0 us)
Async XLA Ops:
  3.8 31.4 %copy-start.1 = (bf16[1,1536,128]{2,1,0:T(8,128)(2,1)S(1)}, bf16[1,1536,128]{2,1,0:T(8,128)(2,1)}, u32[]{:S(2)}) copy-start(bf16[1,1536,128]{2,1,0:T(8,128)(2,1)} %param.8) | copy-start | bytes 1179652
  3.8 150.3 %all-to-all-start = ((bf16[128,2,5632]{2,1,0:T(2,128)(2,1)}), bf16[128,2,5632]{2,1,0:T(2,128)(2,1)S(1)}, u32[]{:S(2)}, u32[]{:S(2)}) async-start(bf16[128,2,5632]{2,1,0:T(2,128)(2,1)} %pack.1), calls=%async_computation | async-start | bytes 5767168 | tf_op jit(solution)/shard_map/all_to_all | solution.py:139
  24.5 115.0 %copy-start = (bf16[1,4096,256]{2,1,0:T(8,128)(2,1)S(1)}, bf16[1,4096,256]{2,1,0:T(8,128)(2,1)}, u32[]{:S(2)}) copy-start(bf16[1,4096,256]{2,1,0:T(8,128)(2,1)} %param.9) | copy-start | bytes 6291460
  24.5 115.0 %collective-permute-start.3 = (bf16[4096,256]{1,0:T(8,128)(2,1)}, bf16[4096,256]{1,0:T(8,128)(2,1)S(1)}, u32[]{:S(2)}, u32[]{:S(2)}) collective-permute-start(bf16[4096,256]{1,0:T(8,128)(2,1)} %bitcast.3), channel_id=1, source_target_pairs={{0,1},{1,2},{2,3},{3,0},{4,5},{5,6},{6,7},{7,4},{8,9},{9,10},{10,1... | collective-permute-start | bytes 6291464 | tf_op jit(solution)/shard_map/ppermute | solution.py:22
  27.8 111.7 %collective-permute-start.4 = (bf16[4096,256]{1,0:T(8,128)(2,1)}, bf16[4096,256]{1,0:T(8,128)(2,1)S(1)}, u32[]{:S(2)}, u32[]{:S(2)}) collective-permute-start(bf16[4096,256]{1,0:T(8,128)(2,1)} %bitcast.4), channel_id=1, source_target_pairs={{0,2},{1,3},{2,0},{3,1},{4,6},{5,7},{6,4},{7,5},{8,10},{9,11},{10,... | collective-permute-start | bytes 6291464 | tf_op jit(solution)/shard_map/ppermute | solution.py:22
  32.2 107.3 %collective-permute-start.5 = (bf16[4096,256]{1,0:T(8,128)(2,1)}, bf16[4096,256]{1,0:T(8,128)(2,1)S(1)}, u32[]{:S(2)}, u32[]{:S(2)}) collective-permute-start(bf16[4096,256]{1,0:T(8,128)(2,1)} %bitcast.5), channel_id=1, source_target_pairs={{0,3},{1,0},{2,1},{3,2},{4,7},{5,4},{6,5},{7,6},{8,11},{9,8},{10,9... | collective-permute-start | bytes 6291464 | tf_op jit(solution)/shard_map/ppermute | solution.py:22
  35.2 92.4 %collective-permute-start = (bf16[1536,128]{1,0:T(8,128)(2,1)S(1)}, bf16[1536,128]{1,0:T(8,128)(2,1)S(1)}, u32[]{:S(2)}, u32[]{:S(2)}) collective-permute-start(bf16[1536,128]{1,0:T(8,128)(2,1)S(1)} %bitcast.7), channel_id=1, source_target_pairs={{0,1},{1,2},{2,3},{3,0},{4,5},{5,6},{6,7},{7,4},{8,9},{9,10},{10,1... | collective-permute-start | bytes 1179656 | tf_op jit(solution)/shard_map/ppermute | solution.py:22
  37.5 99.6 %collective-permute-start.1 = (bf16[1536,128]{1,0:T(8,128)(2,1)S(1)}, bf16[1536,128]{1,0:T(8,128)(2,1)S(1)}, u32[]{:S(2)}, u32[]{:S(2)}) collective-permute-start(bf16[1536,128]{1,0:T(8,128)(2,1)S(1)} %bitcast.8), channel_id=1, source_target_pairs={{0,2},{1,3},{2,0},{3,1},{4,6},{5,7},{6,4},{7,5},{8,10},{9,11},{10,... | collective-permute-start | bytes 1179656 | tf_op jit(solution)/shard_map/ppermute | solution.py:22
  127.6 10.5 %collective-permute-start.2 = (bf16[1536,128]{1,0:T(8,128)(2,1)S(1)}, bf16[1536,128]{1,0:T(8,128)(2,1)S(1)}, u32[]{:S(2)}, u32[]{:S(2)}) collective-permute-start(bf16[1536,128]{1,0:T(8,128)(2,1)S(1)} %bitcast.9), channel_id=1, source_target_pairs={{0,3},{1,0},{2,1},{3,2},{4,7},{5,4},{6,5},{7,6},{8,11},{9,8},{10,9... | collective-permute-start | bytes 1179656 | tf_op jit(solution)/shard_map/ppermute | solution.py:22
  157.2 18.3 %all-to-all-start.1 = ((bf16[4,256,512]{2,1,0:T(8,128)(2,1)}), bf16[4,256,512]{2,1,0:T(8,128)(2,1)}, u32[]{:S(2)}, u32[]{:S(2)}) async-start(bf16[4,256,512]{2,1,0:T(8,128)(2,1)} %input_squares.1), calls=%async_computation.1 | async-start | bytes 2097152 | tf_op jit(solution)/shard_map/all_to_all | solution.py:160
  166.0 10.8 %collective-permute-start.6 = (bf16[256,256]{1,0:T(8,128)(2,1)S(1)}, bf16[256,256]{1,0:T(8,128)(2,1)S(1)}, u32[]{:S(2)}, u32[]{:S(2)}) collective-permute-start(bf16[256,256]{1,0:T(8,128)(2,1)S(1)} %get-tuple-element.16), channel_id=1, source_target_pairs={{0,3},{1,0},{2,1},{3,2},{4,7},{5,4},{6,5},{7,6},{8,11},{9,8},{10,9... | collective-permute-start | bytes 393224 | tf_op jit(solution)/shard_map/ppermute | solution.py:22
  170.5 7.7 %collective-permute-start.7 = (bf16[256,256]{1,0:T(8,128)(2,1)S(1)}, bf16[256,256]{1,0:T(8,128)(2,1)S(1)}, u32[]{:S(2)}, u32[]{:S(2)}) collective-permute-start(bf16[256,256]{1,0:T(8,128)(2,1)S(1)} %get-tuple-element.17), channel_id=1, source_target_pairs={{0,2},{1,3},{2,0},{3,1},{4,6},{5,7},{6,4},{7,5},{8,10},{9,11},{10,... | collective-permute-start | bytes 393224 | tf_op jit(solution)/shard_map/ppermute | solution.py:22
  173.0 7.2 %collective-permute-start.8 = (bf16[256,256]{1,0:T(8,128)(2,1)S(1)}, bf16[256,256]{1,0:T(8,128)(2,1)S(1)}, u32[]{:S(2)}, u32[]{:S(2)}) collective-permute-start(bf16[256,256]{1,0:T(8,128)(2,1)S(1)} %get-tuple-element.18), channel_id=1, source_target_pairs={{0,1},{1,2},{2,3},{3,0},{4,5},{5,6},{6,7},{7,4},{8,9},{9,10},{10,1... | collective-permute-start | bytes 393224 | tf_op jit(solution)/shard_map/ppermute | solution.py:22
